TPU v7x, 128 devices: a whole 4x4x4 slice. The times are simulated.
128 devices in a mesh: gx: 8 (over z_lo, x), gy: 16 (over y, z_hi, core).
Axes of the slice: x: 4, y: 4, z: 4 (z_hi: 2, z_lo: 2; z = z_hi * 2 + z_lo), core: 2. Of those that a mesh axis runs over, the one named last changes fastest.
Arguments:
- displacement: float32 [3, 16, 32, 3, 128], P(None, 'gx', 'gy'), may hold values from -0.15 to 0.15
- velocity: float32 [3, 16, 32, 3, 128], P(None, 'gx', 'gy'), may hold values from -18 to 18
- noise: float32 [4, 3, 16, 32, 3, 128], P(None, None, 'gx', 'gy'), may hold values from -1.7320508 to 1.7320508
- electron_temp: float32 [128, 8, 16], P(('gx', 'gy')), may hold values from 0.5 to 10
- pair_list: int32 [8, 16, 2, 324], P('gx', 'gy'), may hold values from 0 to 26, as said below
- pair_count: int32 [8, 16], P('gx', 'gy'), may hold values from 12 to 324, as said below
Outputs:
- new_displacement: float32 [3, 16, 32, 3, 128], P(None, 'gx', 'gy')
- new_velocity: float32 [3, 16, 32, 3, 128], P(None, 'gx', 'gy')
- electron_final: float32 [128, 8, 16], P(('gx', 'gy'))
Inputs may be any that keep to these rules, and one draw needn't show every extreme that they name: `pair_list`: in each brick the first pair_count entries name distinct (tile, code) pairs, the tile in 0 to 11 and the code in 0 to 26; every tile's code 13 is among them. Later entries are not read. `pair_count`: some brick has exactly 324 live entries and some brick exactly 12.
All inputs are finite; a program needn't handle non-finite values.
Results may differ from a plain program's by a relative error of at most 0.0003.
Values sent between devices are 32-bit elements; how exact they have to be, the bound alone decides.
A program may use at most 64 MiB of HBM per device.

v0:
```python
from functools import partial

import jax
import jax.numpy as jnp
from jax import lax
from jax.sharding import PartitionSpec as P

CB = 4
TILE = 128
BXT = 2
BYT = 2
TZ = 3
TILES = 12
STEPS = 4
SUB = 6


lattice_edge = 3.1652
density_cut = 4.400224
embed_scale = 1.896373
pair_cut = 3.25
coef_zero = 47.1346499
coef_one = -33.7665655
coef_two = 6.2541999
time_step = 0.005
atom_mass = 0.0190534
friction = 1.0
heat_capacity = 0.02
diffusion_rate = 0.12


def padded_2(block, sides, width):
    for axis, dim in sides:
        count = lax.axis_size(axis)
        forward = [(i, i + 1) for i in range(count - 1)]
        forward.append((count - 1, 0))
        backward = [(target, source) for source, target in forward]
        low = lax.ppermute(
            lax.slice_in_dim(block, block.shape[dim] - width, None, axis=dim), axis, forward
        )
        high = lax.ppermute(lax.slice_in_dim(block, 0, width, axis=dim), axis, backward)
        block = jnp.concatenate([low, block, high], axis=dim)
    return block


def lattice_sites():
    serial = jnp.arange(TILE, dtype=jnp.int32)
    cell_number = serial // 2
    half_step = (serial % 2).astype(jnp.float32) * 0.5
    corners = jnp.stack([cell_number // (CB * CB), cell_number // CB % CB, cell_number % CB])
    return lattice_edge * (corners.astype(jnp.float32) + half_step[None, :])


def plane_table(plane_total):
    serial = jnp.arange(TILE, dtype=jnp.int32)
    cell_number = serial // 2
    layer = 2 * (cell_number % CB) + serial % 2
    tiles = jnp.arange(TZ, dtype=jnp.int32)
    whole = tiles[:, None] * (2 * CB) + layer[None, :]
    return whole * plane_total // (2 * CB * TZ)


def pair_geometry(window, tile_index, neighbour_code, lattice):
    wide_y = BYT + 2
    depth_t = tile_index % TZ
    inner_y = tile_index // TZ % BYT
    inner_x = tile_index // (TZ * BYT)
    shift_x = neighbour_code // 9
    shift_y = neighbour_code // 3 % 3
    shift_z = neighbour_code % 3
    flattened = window.reshape(window.shape[0], (BXT + 2) * wide_y * TZ, TILE)
    own_index = ((inner_x + 1) * wide_y + inner_y + 1) * TZ + depth_t
    other_index = ((inner_x + shift_x) * wide_y + inner_y + shift_y) * TZ + (
        depth_t + shift_z - 1 + TZ
    ) % TZ
    own_tile = lax.dynamic_index_in_dim(flattened, own_index, 1, keepdims=False)
    other_tile = lax.dynamic_index_in_dim(flattened, other_index, 1, keepdims=False)
    offset = jnp.stack([shift_x - 1, shift_y - 1, shift_z - 1]).astype(jnp.float32) * (
        CB * lattice_edge
    )
    left = lattice + own_tile
    right = lattice + other_tile + offset[:, None]
    delta = left[:, :, None] - right[:, None, :]
    square = jnp.sum(delta * delta, axis=0)
    serial = jnp.arange(TILE, dtype=jnp.int32)
    same_atom = (neighbour_code == 13) & (serial[:, None] == serial[None, :])
    distance = jnp.sqrt(jnp.where(same_atom, 100.0, square))
    return (delta, distance, own_index, other_index)


def density_term(window, lattice, tile_index, neighbour_code):
    delta, distance, own_index, other_index = pair_geometry(
        window, tile_index, neighbour_code, lattice
    )
    dens_gap = distance - density_cut
    return jnp.sum(jnp.where(distance < density_cut, dens_gap * dens_gap, 0.0), axis=1)[None]


def force_term(window, embed_window, lattice, tile_index, neighbour_code):
    delta, distance, own_index, other_index = pair_geometry(
        window, tile_index, neighbour_code, lattice
    )
    flat_embed = embed_window.reshape((BXT + 2) * (BYT + 2) * TZ, TILE)
    own_embed = lax.dynamic_index_in_dim(flat_embed, own_index, 0, keepdims=False)
    other_embed = lax.dynamic_index_in_dim(flat_embed, other_index, 0, keepdims=False)
    pair_gap = distance - pair_cut
    poly = coef_zero + coef_one * distance + coef_two * distance * distance
    pair_slope = jnp.where(
        distance < pair_cut,
        2.0 * pair_gap * poly + pair_gap * pair_gap * (coef_one + 2.0 * coef_two * distance),
        0.0,
    )
    dens_gap = distance - density_cut
    dens_slope = jnp.where(distance < density_cut, 2.0 * dens_gap, 0.0)
    scalar = (pair_slope + (own_embed[:, None] + other_embed[None, :]) * dens_slope) / distance
    return -jnp.sum(scalar[None] * delta, axis=2)


def sweep_pairs(term_fn, channels, pair_table, pair_total):
    initial = jnp.zeros((channels, TILES, TILE), jnp.float32)

    def block_add(block_index, running):
        start = block_index * 27
        chosen = lax.dynamic_slice_in_dim(pair_table, start, 27, 1)
        live = start + jnp.arange(27, dtype=jnp.int32) < pair_total
        terms = jax.vmap(term_fn)(chosen[0], chosen[1])
        terms = jnp.where(live[:, None, None], terms, 0.0)
        return running.at[:, chosen[0]].add(jnp.swapaxes(terms, 0, 1))

    blocks = pair_table.shape[1] // 27
    total = lax.fori_loop(0, blocks, block_add, initial)
    return total.reshape(channels, BXT, BYT, TZ, TILE)


def relax_slab(padded):
    center = padded[1:-1]
    beside_all = padded[2:] + padded[:-2] + jnp.roll(center, 1, 1) + jnp.roll(center, -1, 1)
    beside_all = beside_all + jnp.roll(center, 1, 2) + jnp.roll(center, -1, 2)
    return center + diffusion_rate * (beside_all - 6.0 * center)


def per_device(displacement, velocity, noise, electron_temp, pair_list, pair_count):
    lattice = lattice_sites()
    pair_table = pair_list[0, 0]
    pair_total = pair_count[0, 0]
    positions = displacement
    speeds = velocity
    across_x = lax.axis_size("gx")
    across_y = lax.axis_size("gy")
    owners = across_x * across_y
    slab_depth = electron_temp.shape[0]
    plane_total = slab_depth * owners
    planes = plane_table(plane_total).reshape(-1)
    heat_field = electron_temp
    for step_index in range(STEPS):
        arrived = lax.all_to_all(
            heat_field.reshape(slab_depth, owners),
            ("gx", "gy"),
            split_axis=1,
            concat_axis=0,
            tiled=True,
        )
        column = arrived.reshape(-1)
        column_temp = jnp.take(column, planes).reshape(TZ, TILE)
        local_temp = jnp.broadcast_to(column_temp, (BXT, BYT, TZ, TILE))
        window = padded_2(positions, (("gx", 1), ("gy", 2)), 1)
        density = sweep_pairs(partial(density_term, window, lattice), 1, pair_table, pair_total)
        embed_slope = -embed_scale / (2.0 * jnp.sqrt(density))
        embed_window = padded_2(embed_slope, (("gx", 1), ("gy", 2)), 1)
        force = sweep_pairs(
            partial(force_term, window, embed_window, lattice), 3, pair_table, pair_total
        )
        kicker = (
            jnp.sqrt(2.0 * friction * atom_mass * local_temp / time_step)[None] * noise[step_index]
        )
        speeds = speeds + time_step / atom_mass * (force - friction * atom_mass * speeds + kicker)
        positions = positions + time_step * speeds
        power = friction * atom_mass * time_step * jnp.sum(speeds * speeds, axis=0)
        tile_power = jnp.sum(power, axis=(0, 1)).reshape(-1)
        energy = jnp.zeros((plane_total,), jnp.float32).at[planes].add(tile_power)
        arrived = lax.all_to_all(
            energy.reshape(plane_total, 1), ("gx", "gy"), split_axis=0, concat_axis=1, tiled=True
        )
        heat_field = heat_field + arrived.reshape(slab_depth, across_x, across_y) / heat_capacity
        for sub_index in range(SUB):
            heat_field = relax_slab(padded_2(heat_field, ((("gx", "gy"), 0),), 1))
    return (positions, speeds, heat_field)


def solution(mesh):
    placed = (
        P(None, "gx", "gy", None, None),
        P(None, "gx", "gy", None, None),
        P(None, None, "gx", "gy", None, None),
        P(("gx", "gy"), None, None),
        P("gx", "gy", None, None),
        P("gx", "gy"),
    )
    return jax.shard_map(
        per_device,
        mesh=mesh,
        in_specs=placed,
        out_specs=(
            P(None, "gx", "gy", None, None),
            P(None, "gx", "gy", None, None),
            P(("gx", "gy"), None, None),
        ),
        check_vma=False,
    )
```

profile of v0, /device:TPU:1, one launch (start us, length us, event | category | flops | bytes accessed | tf_op | source)
XLA Modules:
  0.0 1353.8 jit_solution(14480598465837557749)
XLA Ops:
  2.1 11.5 all-to-all-start
  26.9 80.0 %while.148 = (s32[]{:T(128)}, f32[1,12,128]{2,1,0:T(8,128)S(1)}, s32[2,324]{1,0:T(2,128)}, s32[]{:T(128)}, f32[3,128]{1,0:T(4,128)S(1)}, /*index=5*/f32[3,4,4,3,...) while((s32[]{:T(128)}, f32[1,12,128]{2,1,0:T(8,128)S(1)}, ...), condition=%wide.region_4.5_spmd, body=%wide.region_0.4_spmd.sunk | while | flops 6690088 | bytes 4029412 | solution.py:131
  124.5 154.2 %while.152 = (s32[]{:T(128)}, f32[3,12,128]{2,0,1:T(4,128)S(1)}, s32[2,324]{1,0:T(2,128)S(1)}, s32[]{:T(128)}, f32[3,128]{1,0:T(4,128)S(1)}, /*index=5*/f32[3,4,...) while((s32[]{:T(128)}, f32[3,12,128]{2,0,1:T(4,128)S(1)}, ...), condition=%wide.wide.region_9.10_spmd, body=%wide.wide.region_5.9_spmd.sunk | while | flops 18651360 | bytes 7947431 | solution.py:131
  283.5 10.8 all-to-all-start.1
  343.7 7.4 collective-permute-start.11
  354.7 71.8 %while.149 = (s32[]{:T(128)}, f32[1,12,128]{2,1,0:T(8,128)S(1)}, s32[2,324]{1,0:T(2,128)S(1)}, s32[]{:T(128)}, f32[3,128]{1,0:T(4,128)S(1)}, /*index=5*/f32[3,4,...) while((s32[]{:T(128)}, f32[1,12,128]{2,1,0:T(8,128)S(1)}, ...), condition=%wide.region_14.16_spmd, body=%wide.region_10.15_spmd.sunk | while | flops 6690088 | bytes 4029412 | solution.py:131
  427.5 11.6 all-to-all-start.2
  439.1 9.4 all-to-all-done.2
  460.1 154.2 %while.153 = (s32[]{:T(128)}, f32[3,12,128]{2,0,1:T(4,128)S(1)}, s32[2,324]{1,0:T(2,128)S(1)}, s32[]{:T(128)}, f32[3,128]{1,0:T(4,128)S(1)}, /*index=5*/f32[3,4,...) while((s32[]{:T(128)}, f32[3,12,128]{2,0,1:T(4,128)S(1)}, ...), condition=%wide.wide.region_19.21_spmd, body=%wide.wide.region_15.20_spmd.sunk | while | flops 18651360 | bytes 7947431 | solution.py:131
  619.0 8.8 all-to-all-start.3
  677.1 7.4 collective-permute-start.31
  687.8 71.8 %while.150 = (s32[]{:T(128)}, f32[1,12,128]{2,1,0:T(8,128)S(1)}, s32[2,324]{1,0:T(2,128)S(1)}, s32[]{:T(128)}, f32[3,128]{1,0:T(4,128)S(1)}, /*index=5*/f32[3,4,...) while((s32[]{:T(128)}, f32[1,12,128]{2,1,0:T(8,128)S(1)}, ...), condition=%wide.region_27.29_spmd, body=%wide.region_23.28_spmd.sunk | while | flops 6690088 | bytes 4029412 | solution.py:131
  760.6 12.0 all-to-all-start.4
  772.6 9.4 all-to-all-done.4
  793.6 154.2 %while.154 = (s32[]{:T(128)}, f32[3,12,128]{2,0,1:T(4,128)S(1)}, s32[2,324]{1,0:T(2,128)S(1)}, s32[]{:T(128)}, f32[3,128]{1,0:T(4,128)S(1)}, /*index=5*/f32[3,4,...) while((s32[]{:T(128)}, f32[3,12,128]{2,0,1:T(4,128)S(1)}, ...), condition=%wide.wide.region_32.34_spmd, body=%wide.wide.region_28.33_spmd.sunk | while | flops 18651360 | bytes 7947431 | solution.py:131
  952.5 8.8 all-to-all-start.5
  993.1 7.5 collective-permute-start.62
  1010.9 7.4 collective-permute-start.51
  1021.6 71.8 %while.151 = (s32[]{:T(128)}, f32[1,12,128]{2,1,0:T(8,128)S(1)}, s32[2,324]{1,0:T(2,128)S(1)}, s32[]{:T(128)}, f32[3,128]{1,0:T(4,128)S(1)}, /*index=5*/f32[3,4,...) while((s32[]{:T(128)}, f32[1,12,128]{2,1,0:T(8,128)S(1)}, ...), condition=%wide.region_40.42_spmd, body=%wide.region_36.41_spmd.sunk | while | flops 6690088 | bytes 4029412 | solution.py:131
  1094.4 11.7 all-to-all-start.6
  1106.1 9.4 all-to-all-done.6
  1127.0 154.2 %while.155 = (s32[]{:T(128)}, f32[3,12,128]{2,0,1:T(4,128)S(1)}, s32[2,324]{1,0:T(2,128)S(1)}, s32[]{:T(128)}, f32[3,128]{1,0:T(4,128)S(1)}, /*index=5*/f32[3,4,...) while((s32[]{:T(128)}, f32[3,12,128]{2,0,1:T(4,128)S(1)}, ...), condition=%wide.wide.region_45.47_spmd, body=%wide.wide.region_41.46_spmd.sunk | while | flops 18651360 | bytes 7947431 | solution.py:131
  1285.9 9.0 all-to-all-start.7
  1296.2 8.2 all-to-all-done.7
  (2154 shorter events, 1193.7 us)
Async XLA Ops:
  2.1 105.0 %all-to-all-start = ((f32[1,128,1]{2,0,1:T(1,128)}), f32[1,128,1]{2,0,1:T(1,128)S(1)}, u32[]{:S(2)}, u32[]{:S(2)}) async-start(f32[1,128,1]{2,0,1:T(1,128)} %all_to_all.96), calls=%async_computation | async-start | bytes 131072 | tf_op jit(solution)/shard_map/all_to_all | solution.py:156
  283.5 20.3 %all-to-all-start.1 = ((f32[128,1,1]{2,1,0:T(1,128)}), f32[128,1,1]{2,1,0:T(1,128)S(1)}, u32[]{:S(2)}, u32[]{:S(2)}) async-start(f32[128,1,1]{2,1,0:T(1,128)} %copy.165), calls=%async_computation.1 | async-start | bytes 131072 | tf_op jit(solution)/shard_map/all_to_all | solution.py:181
  294.4 49.3 %collective-permute-start.9 = (f32[3,1,2,3,128]{4,0,3,2,1:T(4,128)S(1)}, f32[3,1,2,3,128]{4,0,3,2,1:T(4,128)S(1)}, u32[]{:S(2)}, u32[]{:S(2)}) collective-permute-start(f32[3,1,2,3,128]{4,0,3,2,1:T(4,128)S(1)} %get-tuple-element.2521), channel_id=1, source_target_pairs={{16,0},{32,16},{48,32},{64,48},{80,64},{96,80},{112,96},{0,112},{1... | collective-permute-start | bytes 27656 | tf_op jit(solution)/shard_map/ppermute | solution.py:41
  298.1 45.6 %collective-permute-start.8 = (f32[3,1,2,3,128]{4,0,3,2,1:T(4,128)S(1)}, f32[3,1,2,3,128]{4,0,3,2,1:T(4,128)S(1)}, u32[]{:S(2)}, u32[]{:S(2)}) collective-permute-start(f32[3,1,2,3,128]{4,0,3,2,1:T(4,128)S(1)} %get-tuple-element.2520), channel_id=1, source_target_pairs={{0,16},{16,32},{32,48},{48,64},{64,80},{80,96},{96,112},{112,0},{1... | collective-permute-start | bytes 27656 | tf_op jit(solution)/shard_map/ppermute | solution.py:38
  343.7 10.9 collective-permute-start.11
  351.3 75.3 %collective-permute-start.26 = (f32[1,8,16]{2,1,0:T(8,128)S(1)}, f32[1,8,16]{2,1,0:T(8,128)S(1)}, u32[]{:S(2)}, u32[]{:S(2)}) collective-permute-start(f32[1,8,16]{2,1,0:T(8,128)S(1)} %fusion.221), channel_id=1, source_target_pairs={{1,0},{2,1},{3,2},{4,3},{5,4},{6,5},{7,6},{8,7},{9,8},{10,9},{11,1... | collective-permute-start | bytes 1544 | tf_op jit(solution)/shard_map/ppermute | solution.py:41
  351.8 74.8 %collective-permute-start.27 = (f32[1,8,16]{2,1,0:T(8,128)S(1)}, f32[1,8,16]{2,1,0:T(8,128)S(1)}, u32[]{:S(2)}, u32[]{:S(2)}) collective-permute-start(f32[1,8,16]{2,1,0:T(8,128)S(1)} %fusion.221), channel_id=1, source_target_pairs={{0,1},{1,2},{2,3},{3,4},{4,5},{5,6},{6,7},{7,8},{8,9},{9,10},{10,1... | collective-permute-start | bytes 1544 | tf_op jit(solution)/shard_map/ppermute | solution.py:38
  426.5 26.9 %collective-permute-start.12 = (f32[1,1,2,3,128]{4,0,3,2,1:T(1,128)S(1)}, f32[1,1,2,3,128]{4,0,3,2,1:T(1,128)S(1)}, u32[]{:S(2)}, u32[]{:S(2)}) collective-permute-start(f32[1,1,2,3,128]{4,0,3,2,1:T(1,128)S(1)} %get-tuple-element.2537), channel_id=1, source_target_pairs={{0,16},{16,32},{32,48},{48,64},{64,80},{80,96},{96,112},{112,0},{1... | collective-permute-start | bytes 9224 | tf_op jit(solution)/shard_map/ppermute | solution.py:38
  427.5 21.1 %all-to-all-start.2 = ((f32[1,128,1]{2,0,1:T(1,128)}), f32[1,128,1]{2,0,1:T(1,128)S(1)}, u32[]{:S(2)}, u32[]{:S(2)}) async-start(f32[1,128,1]{2,0,1:T(1,128)} %all_to_all.97), calls=%async_computation.2 | async-start | bytes 131072 | tf_op jit(solution)/shard_map/all_to_all | solution.py:156
  619.0 18.2 %all-to-all-start.3 = ((f32[128,1,1]{2,1,0:T(1,128)}), f32[128,1,1]{2,1,0:T(1,128)S(1)}, u32[]{:S(2)}, u32[]{:S(2)}) async-start(f32[128,1,1]{2,1,0:T(1,128)} %copy.170), calls=%async_computation.3 | async-start | bytes 131072 | tf_op jit(solution)/shard_map/all_to_all | solution.py:181
  627.8 49.3 %collective-permute-start.29 = (f32[3,1,2,3,128]{4,0,3,2,1:T(4,128)S(1)}, f32[3,1,2,3,128]{4,0,3,2,1:T(4,128)S(1)}, u32[]{:S(2)}, u32[]{:S(2)}) collective-permute-start(f32[3,1,2,3,128]{4,0,3,2,1:T(4,128)S(1)} %get-tuple-element.2519), channel_id=1, source_target_pairs={{16,0},{32,16},{48,32},{64,48},{80,64},{96,80},{112,96},{0,112},{1... | collective-permute-start | bytes 27656 | tf_op jit(solution)/shard_map/ppermute | solution.py:41
  631.5 45.6 %collective-permute-start.28 = (f32[3,1,2,3,128]{4,0,3,2,1:T(4,128)S(1)}, f32[3,1,2,3,128]{4,0,3,2,1:T(4,128)S(1)}, u32[]{:S(2)}, u32[]{:S(2)}) collective-permute-start(f32[3,1,2,3,128]{4,0,3,2,1:T(4,128)S(1)} %get-tuple-element.2518), channel_id=1, source_target_pairs={{0,16},{16,32},{32,48},{48,64},{64,80},{80,96},{96,112},{112,0},{1... | collective-permute-start | bytes 27656 | tf_op jit(solution)/shard_map/ppermute | solution.py:38
  684.5 75.2 %collective-permute-start.46 = (f32[1,8,16]{2,1,0:T(8,128)S(1)}, f32[1,8,16]{2,1,0:T(8,128)S(1)}, u32[]{:S(2)}, u32[]{:S(2)}) collective-permute-start(f32[1,8,16]{2,1,0:T(8,128)S(1)} %fusion.257), channel_id=1, source_target_pairs={{1,0},{2,1},{3,2},{4,3},{5,4},{6,5},{7,6},{8,7},{9,8},{10,9},{11,1... | collective-permute-start | bytes 1544 | tf_op jit(solution)/shard_map/ppermute | solution.py:41
  685.0 74.7 %collective-permute-start.47 = (f32[1,8,16]{2,1,0:T(8,128)S(1)}, f32[1,8,16]{2,1,0:T(8,128)S(1)}, u32[]{:S(2)}, u32[]{:S(2)}) collective-permute-start(f32[1,8,16]{2,1,0:T(8,128)S(1)} %fusion.257), channel_id=1, source_target_pairs={{0,1},{1,2},{2,3},{3,4},{4,5},{5,6},{6,7},{7,8},{8,9},{9,10},{10,1... | collective-permute-start | bytes 1544 | tf_op jit(solution)/shard_map/ppermute | solution.py:38
  759.7 27.3 %collective-permute-start.32 = (f32[1,1,2,3,128]{4,0,3,2,1:T(1,128)S(1)}, f32[1,1,2,3,128]{4,0,3,2,1:T(1,128)S(1)}, u32[]{:S(2)}, u32[]{:S(2)}) collective-permute-start(f32[1,1,2,3,128]{4,0,3,2,1:T(1,128)S(1)} %get-tuple-element.2535), channel_id=1, source_target_pairs={{0,16},{16,32},{32,48},{48,64},{64,80},{80,96},{96,112},{112,0},{1... | collective-permute-start | bytes 9224 | tf_op jit(solution)/shard_map/ppermute | solution.py:38
  760.6 21.4 %all-to-all-start.4 = ((f32[1,128,1]{2,0,1:T(1,128)}), f32[1,128,1]{2,0,1:T(1,128)S(1)}, u32[]{:S(2)}, u32[]{:S(2)}) async-start(f32[1,128,1]{2,0,1:T(1,128)} %all_to_all.98), calls=%async_computation.4 | async-start | bytes 131072 | tf_op jit(solution)/shard_map/all_to_all | solution.py:156
  952.5 18.2 %all-to-all-start.5 = ((f32[128,1,1]{2,1,0:T(1,128)}), f32[128,1,1]{2,1,0:T(1,128)S(1)}, u32[]{:S(2)}, u32[]{:S(2)}) async-start(f32[128,1,1]{2,1,0:T(1,128)} %copy.175), calls=%async_computation.5 | async-start | bytes 131072 | tf_op jit(solution)/shard_map/all_to_all | solution.py:181
  961.3 49.6 %collective-permute-start.49 = (f32[3,1,2,3,128]{4,0,3,2,1:T(4,128)S(1)}, f32[3,1,2,3,128]{4,0,3,2,1:T(4,128)S(1)}, u32[]{:S(2)}, u32[]{:S(2)}) collective-permute-start(f32[3,1,2,3,128]{4,0,3,2,1:T(4,128)S(1)} %get-tuple-element.2517), channel_id=1, source_target_pairs={{16,0},{32,16},{48,32},{64,48},{80,64},{96,80},{112,96},{0,112},{1... | collective-permute-start | bytes 27656 | tf_op jit(solution)/shard_map/ppermute | solution.py:41
  965.0 45.8 %collective-permute-start.48 = (f32[3,1,2,3,128]{4,0,3,2,1:T(4,128)S(1)}, f32[3,1,2,3,128]{4,0,3,2,1:T(4,128)S(1)}, u32[]{:S(2)}, u32[]{:S(2)}) collective-permute-start(f32[3,1,2,3,128]{4,0,3,2,1:T(4,128)S(1)} %get-tuple-element.2516), channel_id=1, source_target_pairs={{0,16},{16,32},{32,48},{48,64},{64,80},{80,96},{96,112},{112,0},{1... | collective-permute-start | bytes 27656 | tf_op jit(solution)/shard_map/ppermute | solution.py:38
  1018.3 75.2 %collective-permute-start.66 = (f32[1,8,16]{2,1,0:T(8,128)S(1)}, f32[1,8,16]{2,1,0:T(8,128)S(1)}, u32[]{:S(2)}, u32[]{:S(2)}) collective-permute-start(f32[1,8,16]{2,1,0:T(8,128)S(1)} %fusion.293), channel_id=1, source_target_pairs={{1,0},{2,1},{3,2},{4,3},{5,4},{6,5},{7,6},{8,7},{9,8},{10,9},{11,1... | collective-permute-start | bytes 1544 | tf_op jit(solution)/shard_map/ppermute | solution.py:41
  1018.8 74.7 %collective-permute-start.67 = (f32[1,8,16]{2,1,0:T(8,128)S(1)}, f32[1,8,16]{2,1,0:T(8,128)S(1)}, u32[]{:S(2)}, u32[]{:S(2)}) collective-permute-start(f32[1,8,16]{2,1,0:T(8,128)S(1)} %fusion.293), channel_id=1, source_target_pairs={{0,1},{1,2},{2,3},{3,4},{4,5},{5,6},{6,7},{7,8},{8,9},{9,10},{10,1... | collective-permute-start | bytes 1544 | tf_op jit(solution)/shard_map/ppermute | solution.py:38
  1093.4 27.0 %collective-permute-start.52 = (f32[1,1,2,3,128]{4,0,3,2,1:T(1,128)S(1)}, f32[1,1,2,3,128]{4,0,3,2,1:T(1,128)S(1)}, u32[]{:S(2)}, u32[]{:S(2)}) collective-permute-start(f32[1,1,2,3,128]{4,0,3,2,1:T(1,128)S(1)} %get-tuple-element.2533), channel_id=1, source_target_pairs={{0,16},{16,32},{32,48},{48,64},{64,80},{80,96},{96,112},{112,0},{1... | collective-permute-start | bytes 9224 | tf_op jit(solution)/shard_map/ppermute | solution.py:38
  1094.4 21.1 %all-to-all-start.6 = ((f32[1,128,1]{2,0,1:T(1,128)}), f32[1,128,1]{2,0,1:T(1,128)S(1)}, u32[]{:S(2)}, u32[]{:S(2)}) async-start(f32[1,128,1]{2,0,1:T(1,128)} %all_to_all.99), calls=%async_computation.6 | async-start | bytes 131072 | tf_op jit(solution)/shard_map/all_to_all | solution.py:156
  1285.9 18.4 %all-to-all-start.7 = ((f32[128,1,1]{2,1,0:T(1,128)}), f32[128,1,1]{2,1,0:T(1,128)S(1)}, u32[]{:S(2)}, u32[]{:S(2)}) async-start(f32[128,1,1]{2,1,0:T(1,128)} %copy.179), calls=%async_computation.7 | async-start | bytes 131072 | tf_op jit(solution)/shard_map/all_to_all | solution.py:181
  (72 other events, 799.8 us)
where the time goes:
time: 1370 us; the launch traced here: 1350 us
  other arithmetic  711 us (52%)
  starting transfers between devices  294 us (21%)
  local copies, waits for them, and re-layouts  248 us (18%)
  waiting for transfers between devices  90.3 us (7%)
    ppermute x40, starting transfers between devices, padded_2(): lax.ppermute(lax.slice_in_dim(block, 0, width, axis=dim), axis, backward)  182 us
    reduce_sum x96, other arithmetic, pair_geometry(): square = jnp.sum(delta * delta, axis=0)  166 us
    reduce_sum x48, other arithmetic, force_term(): return -jnp.sum(scalar[None] * delta, axis=2)  151 us
    scatter-add x96, other arithmetic, block_add(): return running.at[:, chosen[0]].add(jnp.swapaxes(terms, 0, 1))  119 us
    div x48, other arithmetic, force_term(): (pair_slope + (own_embed[:, None] + other_embed[None, :]) * dens_slope) /...  109 us
    gather x96, local copies, waits for them, and re-layouts, pair_geometry(): own_tile = lax.dynamic_index_in_dim(flattened, own_index, 1, keepdims=False)  64.7 us
    gather x96, local copies, waits for them, and re-layouts, pair_geometry(): lax.dynamic_index_in_dim(flattened, other_index, 1, keepdims=False)  64.6 us
    lt x96, other arithmetic, block_add(): live = start + jnp.arange(27, dtype=jnp.int32) < pair_total  62.8 us
  transfers between devices with their start and end apart: 88, of which 57 were waited for; matrix products, arithmetic and copies ran while one was open for 24% of the time, Pallas kernels for 0%

commit v1 on v0

v1 whole, which is shorter than its diff:
```python
from functools import partial

import jax
import jax.numpy as jnp
import numpy as np
from jax import lax
from jax.experimental import pallas as pl
from jax.experimental.pallas import tpu as pltpu
from jax.sharding import PartitionSpec as P

MESH = pl.DeviceIdType.MESH
NGX, NGY = 8, 16
TZ, TILE, TILES, STEPS, SUB = 3, 128, 12, 4, 6
PAIRS = 324

EDGE = 3.1652
RC = 4.400224
EMBED = 1.896373
RP = 3.25
C0, C1, C2 = 47.1346499, -33.7665655, 6.2541999
DT = 0.005
MASS = 0.0190534
HEAT = 0.02
RATE = 0.12

F32 = jnp.float32
PAD = 16
ROWS = 48
FLAT = PAD + ROWS + PAD

OFFSETS = sorted(
    (
        (nx, ny, nz)
        for nx in range(-3, 4)
        for ny in range(-3, 4)
        for nz in range(-3, 4)
        if nx % 2 == ny % 2 == nz % 2 and 0 < nx * nx + ny * ny + nz * nz <= 12
    ),
    key=lambda n: (n[0] ** 2 + n[1] ** 2 + n[2] ** 2 > 8, n[1], n[2], n[0]),
)
NEAR = 26
NEAR_LIMIT = 0.42**2
FAR_LIMIT = 0.96**2
SIDES = [(a, b) for a in (-1, 0, 1) for b in (-1, 0, 1) if (a, b) != (0, 0)]
HOPS = sorted(
    (
        (dx, dy, dz, dc)
        for dx in range(4)
        for dy in range(4)
        for dz in range(4)
        for dc in range(2)
        if (dx, dy, dz, dc) != (0, 0, 0, 0)
    ),
    key=lambda d: -sum(min(v, 4 - v) for v in d[:3]) * 2 - d[3],
)


def lane_tables():
    s = np.arange(TILE)
    cx, cy, hz = s // 32, s // 8 % 4, s % 8
    b = hz % 2
    source, code = [], []
    for nx, ny, nz in OFFSETS:
        odd = nx % 2
        dx = (nx - odd) // 2 + odd * b
        dy = (ny - odd) // 2 + odd * b
        source.append((cx + dx) % 4 * 32 + (cy + dy) % 4 * 8 + (hz + nz) % 8)
        code.append(9 * ((cx + dx) // 4 + 1) + 3 * ((cy + dy) // 4 + 1) + (hz + nz) // 8 + 1)
    table = np.stack(source + code).astype(np.int32)
    return np.ascontiguousarray(np.broadcast_to(table[:, None, :], (2 * len(OFFSETS), 8, TILE)))


def plane_tables():
    s = np.arange(TILE)
    layer = np.arange(8)[:, None] % 3 * 8 + s[None, :] % 8
    plane = layer * 128 // 24
    back = np.zeros((8, TILE), np.int32)
    live = np.zeros((8, TILE), np.int32)
    for L in range(24):
        back[L // 8, L * 128 // 24] = L % 8
        live[L // 8, L * 128 // 24] = 1
    return np.stack([plane, back, live]).astype(np.int32)


def spread(x, index):
    return jnp.take_along_axis(x, index, axis=1, mode="promise_in_bounds")


def body(
    u_in, v_in, noise, heat_in, pairs, count, lanes, planes,
    u_out, v_out, heat_out, flag_out,
    own, arrive, grid, row, win, zed, wye, mask, live_win, vel, kick, field,
    halo_send, halo_recv, all_send, all_recv, junk,
):
    mx, my = lax.axis_index("gx"), lax.axis_index("gy")
    x, zl = lax.rem(mx, 4), mx // 4
    y, zh, core = my // 4, lax.rem(my // 2, 2), lax.rem(my, 2)
    z = zh * 2 + zl
    xs = [lax.rem(x + d, 4) for d in range(4)]
    ys = [lax.rem(y + d, 4) for d in range(4)]
    zs = [lax.rem(z + d, 4) for d in range(4)]
    cs = [lax.rem(core + d, 2) for d in range(2)]
    gxs = {(dx, dz): lax.rem(zs[dz], 2) * 4 + xs[dx] for dx in range(4) for dz in range(4)}
    gys = {
        (dy, dz, dc): ys[dy] * 4 + zs[dz] // 2 * 2 + cs[dc]
        for dy in range(4) for dz in range(4) for dc in range(2)
    }
    peers = [(gxs[dx, dz], gys[dy, dz, dc]) for dx, dy, dz, dc in HOPS]
    sides = [(lax.rem(mx + a + NGX, NGX), lax.rem(my + b + NGY, NGY)) for a, b in SIDES]

    barrier = pltpu.get_barrier_semaphore()
    for peer in peers:
        pl.semaphore_signal(barrier, inc=1, device_id=peer, device_id_type=MESH)

    rows8 = lax.broadcasted_iota(jnp.int32, (8, TILE), 0)
    lane8 = lax.broadcasted_iota(jnp.int32, (8, TILE), 1)
    inside = rows8 < 6

    zero8 = jnp.zeros((8, TILE), F32)
    for k in range(4):
        win[k, 0:PAD] = jnp.zeros((PAD, TILE), F32)
        win[k, PAD + ROWS : FLAT] = jnp.zeros((PAD, TILE), F32)
        for ix in range(2):
            own[0, k, ix] = zero8
    for k in range(3):
        for ix in range(2):
            vel[k, ix] = zero8
            for iy in range(2):
                own[0, k, ix, 3 * iy : 3 * iy + 3] = u_in[k, ix, iy]
                vel[k, ix, 3 * iy : 3 * iy + 3] = v_in[k, ix, iy]
            for n in range(STEPS):
                kick[n, k, ix] = zero8
                for iy in range(2):
                    kick[n, k, ix, 3 * iy : 3 * iy + 3] = noise[n, k, ix, iy]
    tile_row = lax.broadcasted_iota(jnp.int32, (16, PAIRS), 0)
    slot = lax.broadcasted_iota(jnp.int32, (16, PAIRS), 1)
    tile_id = jnp.where(tile_row % 8 < 6, tile_row // 8 * 6 + tile_row % 8, -1)
    named = (pairs[0, 0, 0:1, :] == tile_id) & (slot < count[0:1, 0:1])
    coded = pairs[0, 0, 1:2, :] == lax.broadcasted_iota(jnp.int32, (TILE, PAIRS), 0)
    live = lax.dot_general(
        jnp.where(named, 1.0, 0.0).astype(jnp.bfloat16),
        jnp.where(coded, 1.0, 0.0).astype(jnp.bfloat16),
        (((1,), (1,)), ((), ())),
        preferred_element_type=F32,
    )
    own[0, 3, 0] = live[0:8]
    own[0, 3, 1] = live[8:16]
    for i in range(NGX):
        row[0, 0:1, NGY * i : NGY * (i + 1)] = heat_in[0, i : i + 1, :]

    pl.semaphore_wait(barrier, len(peers))

    def halo_copies(n, channels):
        copies = []
        for i, (a, b) in enumerate(SIDES):
            if a:
                src = own.at[n, pl.ds(0, channels), (a + 1) // 2]
                dst = arrive.at[n, i, pl.ds(0, channels), 0]
            else:
                src = own.at[n, pl.ds(0, channels)]
                dst = arrive.at[n, i, pl.ds(0, channels)]
            copies.append(
                pltpu.make_async_remote_copy(
                    src_ref=src, dst_ref=dst, send_sem=halo_send.at[n, i], recv_sem=halo_recv.at[n, i],
                    device_id=sides[i], device_id_type=MESH,
                )
            )
        return copies

    def send_all(g):
        src = row.at[g, pl.ds(0, 1)]
        dst = grid.at[g, mx, pl.ds(my, 1)]
        for peer in peers:
            pltpu.make_async_remote_copy(
                src_ref=src, dst_ref=dst, send_sem=all_send.at[g], recv_sem=all_recv.at[g],
                device_id=peer, device_id_type=MESH,
            ).start()
        pltpu.make_async_copy(src, dst, all_recv.at[g]).start()
        pltpu.make_async_copy(src, junk.at[pl.ds(0, 1)], all_send.at[g]).start()

    def wait_all(g):
        pltpu.make_async_copy(grid.at[g], grid.at[g], all_recv.at[g]).wait()
        pltpu.make_async_copy(grid.at[g], grid.at[g], all_send.at[g]).wait()

    def place(n, channel, target):
        for ix in range(2):
            start = PAD + 12 * (ix + 1) + 3
            target[start : start + 6] = own[n, channel, ix, 0:6]
        for i, (a, b) in enumerate(SIDES):
            for ix in range(2) if a == 0 else (0,):
                wx = ix + 1 if a == 0 else (0 if a == 1 else 3)
                start = PAD + 12 * wx
                if b == 0:
                    target[start + 3 : start + 9] = arrive[n, i, channel, ix, 0:6]
                elif b == 1:
                    target[start : start + 3] = arrive[n, i, channel, ix, 3:6]
                else:
                    target[start + 9 : start + 12] = arrive[n, i, channel, ix, 0:3]

    hz, cy, cx = lane8 % 8, lane8 // 8 % 4, lane8 // 32
    target_odd = (hz % 2) == 0

    def carried(cell, n):
        if n % 2 == 0:
            d = n // 2
            return cell < d if d > 0 else cell >= 4 + d
        low, high = (n - 1) // 2, (n + 1) // 2
        if n > 0:
            return (target_odd & (cell < high)) | (~target_odd & (cell < low))
        return (target_odd & (cell >= 4 + high)) | (~target_odd & (cell >= 4 + low))

    sign = lambda n: (n > 0) - (n < 0)
    carry_x = {n: carried(cx, n) for n in (-3, -2, -1, 1, 2, 3)}
    carry_y = {n: carried(cy, n) for n in (-3, -2, -1, 1, 2, 3)}
    carry_z = {n: (hz < n if n > 0 else hz >= 8 + n) for n in (-3, -2, -1, 1, 2, 3)}

    def combos(total):
        found = []
        for nx, ny, nz in OFFSETS[:total]:
            if ny and (ny, nz) not in found:
                found.append((ny, nz))
        return found

    slots = {c: i for i, c in enumerate(combos(len(OFFSETS)))}

    def stages(total, k):
        depths = sorted({nz for _, _, nz in OFFSETS[:total] if nz})
        for block in range(ROWS // 8):
            r = PAD + 8 * block
            t = (rows8 + 8 * block) % 3
            middle = win[k, r : r + 8]
            up = jnp.where(t < 2, win[k, r + 1 : r + 9], win[k, r - 2 : r + 6])
            down = jnp.where(t > 0, win[k, r - 1 : r + 7], win[k, r + 2 : r + 10])
            for nz in depths:
                zed[nz + 3, k, r : r + 8] = jnp.where(carry_z[nz], up if nz > 0 else down, middle)
            zed[3, k, r : r + 8] = middle
        for block in range(ROWS // 8):
            r = PAD + 8 * block
            for ny, nz in combos(total):
                e = r + 3 * sign(ny)
                wye[slots[ny, nz], k, r : r + 8] = jnp.where(
                    carry_y[ny], zed[nz + 3, k, e : e + 8], zed[nz + 3, k, r : r + 8]
                )

    def neighbour(o, k, r):
        nx, ny, nz = OFFSETS[o]
        get = (lambda q: wye[slots[ny, nz], k, q : q + 8]) if ny else (lambda q: zed[nz + 3, k, q : q + 8])
        here = get(r)
        if nx:
            here = jnp.where(carry_x[nx], get(r + 12 * sign(nx)), here)
        return spread(here, lanes[o])

    def pair(o, r, mine):
        nx, ny, nz = OFFSETS[o]
        delta = [
            (mine[k] - (0.5 * EDGE) * n) - neighbour(o, k, r) for k, n in enumerate((nx, ny, nz))
        ]
        square = delta[0] * delta[0] + delta[1] * delta[1] + delta[2] * delta[2]
        inverse = lax.rsqrt(square)
        return delta, square * inverse, inverse

    def step(n, total):
        for k in range(3):
            place(n, k, win.at[k])
        for k in range(3):
            stages(total, k)
        for block in range(ROWS // 8):
            r = PAD + 8 * block
            mine = [win[k, r : r + 8] for k in range(3)]
            density = zero8
            for o in range(total):
                _, distance, _ = pair(o, r, mine)
                gap = jnp.minimum(distance - RC, 0.0)
                density = density + mask[o, 8 * block : 8 * block + 8] * (gap * gap)
            win[3, r : r + 8] = -EMBED * lax.rsqrt(density)
        stages(total, 3)
        forces = []
        for ix in range(2):
            q = 15 + 12 * ix
            r = PAD + q
            mine = [win[k, r : r + 8] for k in range(3)]
            slope = win[3, r : r + 8]
            total_force = [zero8] * 3
            for o in range(total):
                delta, distance, inverse = pair(o, r, mine)
                gap = jnp.minimum(distance - RC, 0.0)
                close = jnp.minimum(distance - RP, 0.0)
                quad = (2 * C0 - RP * C1) + distance * ((3 * C1 - 2 * RP * C2) + (4 * C2) * distance)
                scalar = close * quad + (slope + neighbour(o, 3, r)) * gap
                scalar = scalar * inverse * mask[o, q : q + 8]
                total_force = [f - scalar * d for f, d in zip(total_force, delta)]
            forces.append([jnp.where(inside, f, 0.0) for f in total_force])
        return forces

    def diffuse(t):
        for _ in range(SUB):
            beside = jnp.concatenate([t[1:], t[:1]], axis=0) + jnp.concatenate([t[-1:], t[:-1]], axis=0)
            beside = beside + pltpu.roll(t, 1, 1) + pltpu.roll(t, NGY - 1, 1)
            beside = beside + pltpu.roll(t, 1, 2) + pltpu.roll(t, TILE - 1, 2)
            t = t + RATE * (beside - 6.0 * t)
        return t

    def deposit(g):
        lane3 = lax.broadcasted_iota(jnp.int32, (NGX, NGY, TILE), 2)
        added = jnp.where(lane3 == 1, 0.0, grid[g]) * (1.0 / HEAT)
        field[...] = diffuse(field[...] + added)

    def advance(n, forces):
        column = jnp.broadcast_to(field[mx, pl.ds(my, 1), :], (8, TILE))
        local = spread(column, planes[0])
        push = jnp.sqrt((2.0 * MASS / DT) * local)
        power = zero8
        largest = zero8
        for ix in range(2):
            reach = zero8
            for k in range(3):
                speed = vel[k, ix]
                speed = speed + (DT / MASS) * (forces[ix][k] - MASS * speed + push * kick[n, k, ix])
                vel[k, ix] = speed
                moved = own[n, k, ix] + DT * speed
                own[n + 1, k, ix] = moved
                reach = reach + moved * moved
                power = power + jnp.where(inside, speed * speed, 0.0)
            largest = jnp.maximum(largest, reach)
        return (MASS * DT) * power, largest

    def energies(n, power, largest):
        power = power + pltpu.roll(power, 5, 0)
        for shift in (8, 16, 32, 64):
            power = power + pltpu.roll(power, shift, 1)
        out = jnp.where(planes[2] > 0, spread(power, planes[1]), 0.0)
        out = jnp.sum(out, axis=0, keepdims=True)
        top = jnp.max(jnp.max(jnp.where(inside, largest, 0.0), axis=1, keepdims=True), axis=0, keepdims=True)
        row[n + 1, 0:1] = jnp.where(lane8[0:1] == 1, top, out)

    def full_step(n, total):
        forces = step(n, total)
        wait_all(n)

        @pl.when(n == 0)
        def _():
            field[...] = jnp.transpose(grid[0].reshape(TILE, TILE)).reshape(NGX, NGY, TILE)

        @pl.when(n > 0)
        def _():
            deposit(n)

        power, largest = advance(n, forces)

        @pl.when(n < STEPS - 1)
        def _():
            for c in halo_copies(n + 1, 3):
                c.start()

        energies(n, power, largest)
        send_all(n + 1)

        @pl.when(n < STEPS - 1)
        def _():
            for c in halo_copies(n + 1, 3):
                c.wait_recv()
            for c in halo_copies(n + 1, 3):
                c.wait_send()

    for c in halo_copies(0, 4):
        c.start()
    send_all(0)
    for c in halo_copies(0, 4):
        c.wait_recv()
    for c in halo_copies(0, 4):
        c.wait_send()

    place(0, 3, live_win)
    for block in range(ROWS // 8):
        known = live_win[PAD + 8 * block : PAD + 8 * block + 8]
        for o in range(len(OFFSETS)):
            mask[o, 8 * block : 8 * block + 8] = spread(known, lanes[len(OFFSETS) + o])

    lax.fori_loop(0, 2, lambda n, c: (full_step(n, NEAR), c)[1], 0)
    lax.fori_loop(2, 4, lambda n, c: (full_step(n, len(OFFSETS)), c)[1], 0)

    for k in range(3):
        for ix in range(2):
            for iy in range(2):
                u_out[k, ix, iy] = own[STEPS, k, ix, 3 * iy : 3 * iy + 3]
                v_out[k, ix, iy] = vel[k, ix, 3 * iy : 3 * iy + 3]
    near = jnp.max(jnp.max(grid[1], axis=0), axis=0, keepdims=True)
    far = jnp.maximum(jnp.max(grid[2], axis=0), jnp.max(grid[3], axis=0))
    far = jnp.max(far, axis=0, keepdims=True)
    flag_out[...] = jnp.where((near <= NEAR_LIMIT) & (far <= FAR_LIMIT), 1.0, 0.0)

    wait_all(STEPS)
    deposit(STEPS)
    lane3 = lax.broadcasted_iota(jnp.int32, (NGX, NGY, TILE), 2)
    heat_out[0] = jnp.sum(jnp.where(lane3 == mx * NGY + my, field[...], 0.0), axis=2)


def fast(displacement, velocity, noise, electron_temp, pair_list, pair_count):
    block = (3, 2, 2, TZ, TILE)
    whole = pl.BlockSpec(memory_space=pltpu.VMEM)
    total = len(OFFSETS)
    return pl.pallas_call(
        body,
        out_shape=(
            jax.ShapeDtypeStruct(block, F32),
            jax.ShapeDtypeStruct(block, F32),
            jax.ShapeDtypeStruct((1, NGX, NGY), F32),
            jax.ShapeDtypeStruct((1, TILE), F32),
        ),
        in_specs=[whole] * 8,
        out_specs=(whole,) * 4,
        scratch_shapes=[
            pltpu.VMEM((STEPS + 1, 4, 2, 8, TILE), F32),
            pltpu.VMEM((STEPS, 8, 4, 2, 8, TILE), F32),
            pltpu.VMEM((STEPS + 1, NGX, NGY, TILE), F32),
            pltpu.VMEM((STEPS + 1, 8, TILE), F32),
            pltpu.VMEM((4, FLAT, TILE), F32),
            pltpu.VMEM((7, 4, FLAT, TILE), F32),
            pltpu.VMEM((18, 4, FLAT, TILE), F32),
            pltpu.VMEM((total, ROWS, TILE), F32),
            pltpu.VMEM((FLAT, TILE), F32),
            pltpu.VMEM((3, 2, 8, TILE), F32),
            pltpu.VMEM((STEPS, 3, 2, 8, TILE), F32),
            pltpu.VMEM((NGX, NGY, TILE), F32),
            pltpu.SemaphoreType.DMA((STEPS, 8)),
            pltpu.SemaphoreType.DMA((STEPS, 8)),
            pltpu.SemaphoreType.DMA((STEPS + 1,)),
            pltpu.SemaphoreType.DMA((STEPS + 1,)),
            pltpu.VMEM((8, TILE), F32),
        ],
        compiler_params=pltpu.CompilerParams(
            collective_id=0, has_side_effects=True, vmem_limit_bytes=40 << 20
        ),
    )(
        displacement, velocity, noise, electron_temp, pair_list, pair_count,
        jnp.asarray(lane_tables()), jnp.asarray(plane_tables()),
    )


def padded_2(values, sides, width):
    for axis, dim in sides:
        count = lax.axis_size(axis)
        forward = [(i, (i + 1) % count) for i in range(count)]
        backward = [(target, source) for source, target in forward]
        low = lax.ppermute(lax.slice_in_dim(values, values.shape[dim] - width, None, axis=dim), axis, forward)
        high = lax.ppermute(lax.slice_in_dim(values, 0, width, axis=dim), axis, backward)
        values = jnp.concatenate([low, values, high], axis=dim)
    return values


def lattice_sites():
    serial = jnp.arange(TILE, dtype=jnp.int32)
    cell = serial // 2
    corners = jnp.stack([cell // 16, cell // 4 % 4, cell % 4])
    return EDGE * (corners.astype(F32) + ((serial % 2).astype(F32) * 0.5)[None, :])


def pair_geometry(flat, tile_index, code, lattice):
    t, iy, ix = tile_index % TZ, tile_index // TZ % 2, tile_index // (TZ * 2)
    ex, ey, ez = code // 9, code // 3 % 3, code % 3
    own_index = ((ix + 1) * 4 + iy + 1) * TZ + t
    other_index = ((ix + ex) * 4 + iy + ey) * TZ + (t + ez - 1 + TZ) % TZ
    own_tile = lax.dynamic_index_in_dim(flat, own_index, 1, keepdims=False)
    other_tile = lax.dynamic_index_in_dim(flat, other_index, 1, keepdims=False)
    offset = jnp.stack([ex - 1, ey - 1, ez - 1]).astype(F32) * (4 * EDGE)
    delta = (lattice + own_tile)[:, :, None] - (lattice + other_tile + offset[:, None])[:, None, :]
    square = jnp.sum(delta * delta, axis=0)
    serial = jnp.arange(TILE, dtype=jnp.int32)
    same = (code == 13) & (serial[:, None] == serial[None, :])
    return delta, jnp.sqrt(jnp.where(same, 100.0, square)), own_index, other_index


def density_term(flat, lattice, tile_index, code):
    _, distance, _, _ = pair_geometry(flat, tile_index, code, lattice)
    gap = distance - RC
    return jnp.sum(jnp.where(distance < RC, gap * gap, 0.0), axis=1)[None]


def force_term(flat, embed, lattice, tile_index, code):
    delta, distance, own_index, other_index = pair_geometry(flat, tile_index, code, lattice)
    own_embed = lax.dynamic_index_in_dim(embed, own_index, 0, keepdims=False)
    other_embed = lax.dynamic_index_in_dim(embed, other_index, 0, keepdims=False)
    gap = distance - RP
    poly = C0 + C1 * distance + C2 * distance * distance
    slope = jnp.where(distance < RP, 2.0 * gap * poly + gap * gap * (C1 + 2.0 * C2 * distance), 0.0)
    dens = jnp.where(distance < RC, 2.0 * (distance - RC), 0.0)
    scalar = (slope + (own_embed[:, None] + other_embed[None, :]) * dens) / distance
    return -jnp.sum(scalar[None] * delta, axis=2)


def sweep(term, channels, table, total):
    def visit(i, running):
        entry = lax.dynamic_slice_in_dim(table, i, 1, 1)
        u = entry[0, 0]
        value = jnp.where(i < total, term(u, entry[1, 0]), 0.0)
        old = lax.dynamic_slice_in_dim(running, u, 1, 1)
        return lax.dynamic_update_slice_in_dim(running, old + value[:, None], u, 1)

    running = lax.fori_loop(0, PAIRS, visit, jnp.zeros((channels, TILES, TILE), F32))
    return running.reshape(channels, 2, 2, TZ, TILE)


def slow(displacement, velocity, noise, electron_temp, pair_list, pair_count):
    lattice = lattice_sites()
    table, total = pair_list[0, 0], pair_count[0, 0]
    owners = NGX * NGY
    serial = np.arange(TZ * TILE)
    layer = serial // TILE * 8 + serial % 8
    onehot = jnp.asarray((layer * owners // 24)[:, None] == np.arange(owners)[None, :])
    axes = (("gx", 1), ("gy", 2))

    def one(n, carry):
        positions, speeds, heat = carry
        arrived = lax.all_to_all(heat.reshape(1, owners), ("gx", "gy"), split_axis=1, concat_axis=0, tiled=True)
        local = jnp.sum(jnp.where(onehot, arrived.reshape(1, owners), 0.0), axis=1).reshape(1, 1, 1, TZ, TILE)
        flat = padded_2(positions, axes, 1).reshape(3, 16 * TZ, TILE)
        density = sweep(partial(density_term, flat, lattice), 1, table, total)
        embed = padded_2(-EMBED / (2.0 * jnp.sqrt(density)), axes, 1).reshape(16 * TZ, TILE)
        force = sweep(partial(force_term, flat, embed, lattice), 3, table, total)
        kicker = jnp.sqrt(2.0 * MASS * local / DT) * lax.dynamic_index_in_dim(noise, n, 0, keepdims=False)
        speeds = speeds + DT / MASS * (force - MASS * speeds + kicker)
        positions = positions + DT * speeds
        power = MASS * DT * jnp.sum(speeds * speeds, axis=0)
        power = jnp.sum(power, axis=(0, 1)).reshape(-1, 1)
        energy = jnp.sum(jnp.where(onehot, power, 0.0), axis=0)
        arrived = lax.all_to_all(energy.reshape(owners, 1), ("gx", "gy"), split_axis=0, concat_axis=1, tiled=True)
        heat = heat + arrived.reshape(1, NGX, NGY) / HEAT

        def relax(_, heat):
            padded = padded_2(heat, ((("gx", "gy"), 0),), 1)
            beside = padded[2:] + padded[:-2] + jnp.roll(heat, 1, 1) + jnp.roll(heat, -1, 1)
            beside = beside + jnp.roll(heat, 1, 2) + jnp.roll(heat, -1, 2)
            return heat + RATE * (beside - 6.0 * heat)

        return positions, speeds, lax.fori_loop(0, SUB, relax, heat)

    return lax.fori_loop(0, STEPS, one, (displacement, velocity, electron_temp))


def per_device(*arguments):
    *results, flag = fast(*arguments)
    return lax.cond(flag[0, 1] > 0.5, lambda: tuple(results), lambda: slow(*arguments))


def solution(mesh):
    brick = P(None, "gx", "gy", None, None)
    placed = (
        brick,
        brick,
        P(None, None, "gx", "gy", None, None),
        P(("gx", "gy"), None, None),
        P("gx", "gy", None, None),
        P("gx", "gy"),
    )
    return jax.shard_map(
        per_device, mesh=mesh, in_specs=placed, out_specs=(brick, brick, P(("gx", "gy"), None, None)), check_vma=False
    )
```

time: 1370 us -> 58.3 us (0.04); the launches traced: 1350 us -> 57.9 us
  other arithmetic: 711 us -> 0 us
  starting transfers between devices: 294 us -> 0 us
  local copies, waits for them, and re-layouts: 248 us -> 5.22 us
  waiting for transfers between devices: 90.3 us -> 0 us
  Pallas kernels: 0 us -> 50.5 us
    reduce_sum x200 -> x0, other arithmetic: 366 us -> none  [the longest x96 166 us: pair_geometry(): square = jnp.sum(delta * delta, axis=0)]
    ppermute x80 -> x0, starting transfers between devices: 210 us -> none  [the longest x40 182 us: padded_2(): lax.ppermute(lax.slice_in_dim(block, 0, width, axis=dim), axis, backward)]
    gather x292 -> x0, local copies, waits for them, and re-layouts: 206 us -> none  [the longest x96 64.7 us: pair_geometry(): own_tile = lax.dynamic_index_in_dim(flattened, own_index, 1, keepdims=False)]
    scatter-add x100 -> x0, other arithmetic: 135 us -> none  [the longest x96 119 us: block_add(): return running.at[:, chosen[0]].add(jnp.swapaxes(terms, 0, 1))]
    div x56 -> x0, other arithmetic: 113 us -> none  [the longest x48 109 us: force_term(): (pair_slope + (own_embed[:, None] + other_embed[None, :]) * dens_slope) /...]
    all_to_all x8 -> x0, starting transfers between devices: 84.1 us -> none  [the longest x4 46.7 us: per_device(): lax.all_to_all(heat_field.reshape(slab_depth, owners), ('gx', 'gy'), spli...]
    lt x96 -> x0, other arithmetic: 62.8 us -> none  [block_add(): live = start + jnp.arange(27, dtype=jnp.int32) < pair_total]
    all_to_all x8 -> x0, waiting for transfers between devices: 53.6 us -> none  [the longest x4 28.3 us: per_device(): lax.all_to_all(heat_field.reshape(slab_depth, owners), ('gx', 'gy'), spli...]
  transfers between devices with their start and end apart: 88 -> 0, of which waited for: 57 -> 0; matrix products, arithmetic and copies ran while one was open for 24% -> 0% of each run, Pallas kernels for 0% -> 0%
where the time goes in v1:
time: 58.3 us; the launch traced here: 57.9 us
  Pallas kernels  50.5 us (87%)
  local copies, waits for them, and re-layouts  5.22 us (9%)
  between operations  2.02 us (3%)
    pallas_call x1, Pallas kernels, fast(): pl.pallas_call(body, out_shape=(jax.ShapeDtypeStruct(block, F32), jax.Sha...  50.5 us
    unnamed x16, local copies, waits for them, and re-layouts  3.38 us
    cond x2, local copies, waits for them, and re-layouts, per_device(): lax.cond(flag[0, 1] > 0.5, lambda: tuple(results), lambda: slow(*arguments))  1.23 us

profile of v1, /device:TPU:1, one launch (start us, length us, event | category | flops | bytes accessed | tf_op | source)
XLA Modules:
  0.0 57.9 jit_solution(14633087410105243343)
XLA Ops:
  0.6 0.7 %copy.162.heat_in = f32[1,8,16]{2,1,0:T(8,128)S(1)} copy(f32[1,8,16]{2,1,0:T(8,128)} %param.22) | data formatting | bytes 1024
  1.3 0.0 copy-start.5
  1.3 0.9 %copy.92.noise = f32[4,3,2,2,3,128]{5,4,3,2,1,0:T(4,128)S(1)} copy(f32[4,3,2,2,3,128]{5,3,4,2,1,0:T(2,128)} %param.21) | data formatting | bytes 147456 | tf_op args[2]
  2.2 0.0 copy-done.5
  2.3 0.0 copy-start.6
  2.3 0.7 %copy-done.6 = f32[3,2,2,3,128]{4,2,3,1,0:T(2,128)S(1)} copy-done((f32[3,2,2,3,128]{4,2,3,1,0:T(2,128)S(1)}, f32[3,2,2,3,128]{4,2,3,1,0:T(2,128)}, u32[]{:S(2)}) %copy-start.6) | copy-done | bytes 18456
  3.0 0.0 copy-start.1
  3.0 0.0 copy-start.4
  3.7 0.0 copy-done.1
  3.7 0.0 copy-done.4
  3.7 0.0 copy-start
  3.7 1.0 %copy-done = s32[116,8,128]{2,1,0:T(8,128)S(1)} copy-done((s32[116,8,128]{2,1,0:T(8,128)S(1)}, s32[116,8,128]{2,1,0:T(8,128)}, u32[]{:S(2)}) %copy-start) | copy-done | bytes 475160
  4.7 50.5 %shard_map.113 = (f32[3,2,2,3,128]{4,3,2,1,0:T(4,128)S(1)}, f32[3,2,2,3,128]{4,3,2,1,0:T(4,128)S(1)}, f32[1,8,16]{2,1,0:T(8,128)S(1)}, f32[1,128]{1,0:T(1,128)S(1)}) custom-call(f32[3,2,2,3,128]{4,3,2,1,0:T(4,128)S(1)} %copy.90.u_in, f32[3,2,2,3,128]{4,3,2,1,0:T(4,128)S(1)} %copy.91.v_in, f32[4,3,2,2,3,128]{5,4,3,2,1,0:T(4,128)S(1)} %copy.92.noise, ...), custom_call_target="tpu_custom_call" | custom-call | tf_op jit(solution)/shard_map/pallas_call | solution.py:402
  55.2 0.6 %slice.187 = f32[1,1]{1,0:T(1,128)} slice(f32[1,128]{1,0:T(1,128)S(1)} %get-tuple-element.1076), slice={[0:1], [1:2]} | slice | bytes 8 | tf_op jit(solution)/shard_map/slice | solution.py:542
  56.4 0.2 conditional.1
  56.7 0.0 copy-start.2
  56.7 0.6 %copy.98 = f32[3,2,2,3,128]{4,2,3,1,0:T(2,128)} copy(f32[3,2,2,3,128]{4,0,3,2,1:T(4,128)S(1)} %get-tuple-element.1213) | data formatting | bytes 36864 | tf_op jit(solution)/shard_map/cond | solution.py:542
  57.3 0.0 copy-done.2
  57.3 0.6 %copy.99 = f32[3,2,2,3,128]{4,2,3,1,0:T(2,128)} copy(f32[3,2,2,3,128]{4,0,3,2,1:T(4,128)S(1)} %get-tuple-element.1214) | data formatting | bytes 36864 | tf_op jit(solution)/shard_map/cond | solution.py:542
  (5 shorter events, 0.0 us)
Async XLA Ops:
  1.3 0.9 %copy-start.5 = (f32[3,2,2,3,128]{4,2,3,1,0:T(2,128)S(1)}, f32[3,2,2,3,128]{4,2,3,1,0:T(2,128)}, u32[]{:S(2)}) copy-start(f32[3,2,2,3,128]{4,2,3,1,0:T(2,128)} %param.19) | copy-start | bytes 55300
  2.3 0.7 %copy-start.6 = (f32[3,2,2,3,128]{4,2,3,1,0:T(2,128)S(1)}, f32[3,2,2,3,128]{4,2,3,1,0:T(2,128)}, u32[]{:S(2)}) copy-start(f32[3,2,2,3,128]{4,2,3,1,0:T(2,128)} %param.20) | copy-start | bytes 55300
  3.0 0.7 %copy-start.1 = (s32[3,8,128]{2,1,0:T(8,128)S(1)}, s32[3,8,128]{2,1,0:T(8,128)}, u32[]{:S(2)}) copy-start(s32[3,8,128]{2,1,0:T(8,128)} %constant.774.clone.planes) | copy-start | bytes 36868
  3.0 0.7 %copy-start.4 = (s32[1,1,2,324]{3,2,1,0:T(2,128)S(1)}, s32[1,1,2,324]{3,2,1,0:T(2,128)}, u32[]{:S(2)}) copy-start(s32[1,1,2,324]{3,2,1,0:T(2,128)} %pairs.1) | copy-start | bytes 7780
  3.7 1.0 %copy-start = (s32[116,8,128]{2,1,0:T(8,128)S(1)}, s32[116,8,128]{2,1,0:T(8,128)}, u32[]{:S(2)}) copy-start(s32[116,8,128]{2,1,0:T(8,128)} %constant.773.clone.lanes) | copy-start | bytes 1425412
  56.7 0.6 %copy-start.2 = (f32[1,8,16]{2,1,0:T(8,128)}, f32[1,8,16]{2,1,0:T(8,128)S(1)}, u32[]{:S(2)}) copy-start(f32[1,8,16]{2,1,0:T(8,128)S(1)} %get-tuple-element.1215) | copy-start | bytes 1540

commit v2 on v1

--- a/solution.py
+++ b/solution.py
@@ -24,9 +24,11 @@
 RATE = 0.12
 
 F32 = jnp.float32
+OWN = 24
 PAD = 16
 ROWS = 48
 FLAT = PAD + ROWS + PAD
+FIRST, BLOCKS = 6, 5
 
 OFFSETS = sorted(
     (
@@ -41,6 +43,19 @@
 NEAR = 26
 NEAR_LIMIT = 0.42**2
 FAR_LIMIT = 0.96**2
+
+
+def combos(total):
+    found = []
+    for _, ny, nz in OFFSETS[:total]:
+        if (ny, nz) != (0, 0) and (ny, nz) not in found:
+            found.append((ny, nz))
+    return found
+
+
+SHIFTS = combos(len(OFFSETS))
+SLOT = {c: i for i, c in enumerate(SHIFTS)}
+SLOT[0, 0] = len(SHIFTS)
 SIDES = [(a, b) for a in (-1, 0, 1) for b in (-1, 0, 1) if (a, b) != (0, 0)]
 HOPS = sorted(
     (
@@ -53,33 +68,28 @@
     ),
     key=lambda d: -sum(min(v, 4 - v) for v in d[:3]) * 2 - d[3],
 )
+SOURCE, CODE, PLANE, BACK, HELD = 0, 20, 41, 44, 45
 
 
 def lane_tables():
     s = np.arange(TILE)
-    cx, cy, hz = s // 32, s // 8 % 4, s % 8
-    b = hz % 2
-    source, code = [], []
-    for nx, ny, nz in OFFSETS:
-        odd = nx % 2
-        dx = (nx - odd) // 2 + odd * b
-        dy = (ny - odd) // 2 + odd * b
-        source.append((cx + dx) % 4 * 32 + (cy + dy) % 4 * 8 + (hz + nz) % 8)
-        code.append(9 * ((cx + dx) // 4 + 1) + 3 * ((cy + dy) // 4 + 1) + (hz + nz) // 8 + 1)
-    table = np.stack(source + code).astype(np.int32)
-    return np.ascontiguousarray(np.broadcast_to(table[:, None, :], (2 * len(OFFSETS), 8, TILE)))
-
-
-def plane_tables():
-    s = np.arange(TILE)
-    layer = np.arange(8)[:, None] % 3 * 8 + s[None, :] % 8
-    plane = layer * 128 // 24
-    back = np.zeros((8, TILE), np.int32)
-    live = np.zeros((8, TILE), np.int32)
-    for L in range(24):
-        back[L // 8, L * 128 // 24] = L % 8
-        live[L // 8, L * 128 // 24] = 1
-    return np.stack([plane, back, live]).astype(np.int32)
+    cell, hz = s // 8, s % 8
+    out = []
+    for ny, nz in SHIFTS:
+        dy = (ny - ny % 2) // 2 + ny % 2 * (hz % 2)
+        out.append((cell + dy) % 16 * 8 + (hz + nz) % 8)
+    for ny, nz in SHIFTS + [(0, 0)]:
+        dy = (ny - ny % 2) // 2 + ny % 2 * (hz % 2)
+        out.append(s // 32 * 32 + 9 + 3 * ((cell % 4 + dy) // 4 + 1) + (hz + nz) // 8 + 1)
+    out = [np.broadcast_to(v[None, :], (8, TILE)) for v in out]
+    rows = np.arange(OWN)[:, None] % 3
+    out += list(((rows * 8 + hz[None, :]) * 128 // 24).reshape(3, 8, TILE))
+    back, held = np.zeros((8, TILE)), np.zeros((OWN, TILE))
+    for layer in range(24):
+        back[:, layer * 128 // 24] = layer % 8
+        held[:, layer * 128 // 24] = rows[:, 0] == layer // 8
+    out += [back] + list(held.reshape(3, 8, TILE))
+    return np.stack(out).astype(np.int32)
 
 
 def spread(x, index):
@@ -87,10 +97,11 @@
 
 
 def body(
-    u_in, v_in, noise, heat_in, pairs, count, lanes, planes,
+    u_in, v_in, noise, heat_in, pairs_in, count, tables,
     u_out, v_out, heat_out, flag_out,
-    own, arrive, grid, row, win, zed, wye, mask, live_win, vel, kick, field,
-    halo_send, halo_recv, all_send, all_recv, junk,
+    own, turned, arrive, grid, row, win, shifted, mask, live_win, vel, kick, field,
+    raw, back, heat, pairs, lanes,
+    in_sem, halo_send, halo_recv, all_send, all_recv, junk,
 ):
     mx, my = lax.axis_index("gx"), lax.axis_index("gy")
     x, zl = lax.rem(mx, 4), mx // 4
@@ -112,52 +123,90 @@
     for peer in peers:
         pl.semaphore_signal(barrier, inc=1, device_id=peer, device_id_type=MESH)
 
+    loads = [
+        pltpu.make_async_copy(pairs_in, pairs, in_sem.at[0]),
+        pltpu.make_async_copy(heat_in, heat, in_sem.at[1]),
+        pltpu.make_async_copy(tables, lanes, in_sem.at[2]),
+    ]
+    for ix in range(2):
+        for iy in range(2):
+            spot = pl.ds(3 * ix, 3)
+            at = 3 + 3 * (2 * ix + iy)
+            loads += [
+                pltpu.make_async_copy(u_in.at[:, ix, :, iy], raw.at[iy, pl.ds(0, 3), spot], in_sem.at[at]),
+                pltpu.make_async_copy(v_in.at[:, ix, :, iy], raw.at[iy, pl.ds(3, 3), spot], in_sem.at[at + 1]),
+            ] + [
+                pltpu.make_async_copy(
+                    noise.at[n, :, ix, :, iy], raw.at[iy, pl.ds(6 + 3 * n, 3), spot], in_sem.at[15 + 4 * n + 2 * ix + iy]
+                )
+                for n in range(STEPS)
+            ]
+    for copy in loads:
+        copy.start()
+
     rows8 = lax.broadcasted_iota(jnp.int32, (8, TILE), 0)
     lane8 = lax.broadcasted_iota(jnp.int32, (8, TILE), 1)
-    inside = rows8 < 6
-
+    hz = lane8 % 8
+    odd = hz % 2 == 1
+    inside = (lane8 >= 32) & (lane8 < 96)
     zero8 = jnp.zeros((8, TILE), F32)
+
     for k in range(4):
-        win[k, 0:PAD] = jnp.zeros((PAD, TILE), F32)
-        win[k, PAD + ROWS : FLAT] = jnp.zeros((PAD, TILE), F32)
-        for ix in range(2):
-            own[0, k, ix] = zero8
+        win[k] = jnp.zeros((FLAT, TILE), F32)
+    live_win[...] = jnp.zeros((FLAT, TILE), F32)
+    for i in range(len(SHIFTS)):
+        for k in range(4):
+            shifted[i, k, 0:PAD] = jnp.zeros((PAD, TILE), F32)
+            shifted[i, k, PAD + ROWS : FLAT] = jnp.zeros((PAD, TILE), F32)
+
+    for copy in loads:
+        copy.wait()
+
+    def gathered(c, cell):
+        low, high = raw[0, c], raw[1, c]
+        low = low if cell == 1 else pltpu.roll(low, (32 * (1 - cell)) % TILE, 1)
+        high = high if cell == 2 else pltpu.roll(high, (32 * (2 - cell)) % TILE, 1)
+        return jnp.where(lane8 < 64, low, high)
+
+    def unpack(c, target):
+        for cell in range(4):
+            value = jnp.where(inside, gathered(c, cell), 0.0)
+            for ix in range(2):
+                start = (4 * ix + cell) * 3
+                target[start : start + 3] = value[3 * ix : 3 * ix + 3]
+
     for k in range(3):
-        for ix in range(2):
-            vel[k, ix] = zero8
-            for iy in range(2):
-                own[0, k, ix, 3 * iy : 3 * iy + 3] = u_in[k, ix, iy]
-                vel[k, ix, 3 * iy : 3 * iy + 3] = v_in[k, ix, iy]
-            for n in range(STEPS):
-                kick[n, k, ix] = zero8
-                for iy in range(2):
-                    kick[n, k, ix, 3 * iy : 3 * iy + 3] = noise[n, k, ix, iy]
-    tile_row = lax.broadcasted_iota(jnp.int32, (16, PAIRS), 0)
-    slot = lax.broadcasted_iota(jnp.int32, (16, PAIRS), 1)
-    tile_id = jnp.where(tile_row % 8 < 6, tile_row // 8 * 6 + tile_row % 8, -1)
-    named = (pairs[0, 0, 0:1, :] == tile_id) & (slot < count[0:1, 0:1])
-    coded = pairs[0, 0, 1:2, :] == lax.broadcasted_iota(jnp.int32, (TILE, PAIRS), 0)
-    live = lax.dot_general(
+        unpack(k, own.at[0, k])
+        unpack(3 + k, vel.at[k])
+
+    p_row = lax.broadcasted_iota(jnp.int32, (OWN, PAIRS), 0)
+    p_lane = lax.broadcasted_iota(jnp.int32, (TILE, PAIRS), 0)
+    slot = lax.broadcasted_iota(jnp.int32, (OWN, PAIRS), 1)
+    tile, code = pairs[0, 0, 0:1, :], pairs[0, 0, 1:2, :]
+    named = (tile // 6 * 3 + tile % 3 == p_row // 12 * 3 + p_row % 3) & (slot < count[0:1, 0:1])
+    coded = tile // 3 % 2 * 32 + 32 + code == p_lane
+    own[0, 3] = lax.dot_general(
         jnp.where(named, 1.0, 0.0).astype(jnp.bfloat16),
         jnp.where(coded, 1.0, 0.0).astype(jnp.bfloat16),
         (((1,), (1,)), ((), ())),
         preferred_element_type=F32,
     )
-    own[0, 3, 0] = live[0:8]
-    own[0, 3, 1] = live[8:16]
+    for k in range(4):
+        turned[0, k] = pltpu.roll(own[0, k], 64, 1)
     for i in range(NGX):
-        row[0, 0:1, NGY * i : NGY * (i + 1)] = heat_in[0, i : i + 1, :]
+        row[0, 0:1, NGY * i : NGY * (i + 1)] = heat[0, i : i + 1, :]
 
     pl.semaphore_wait(barrier, len(peers))
 
     def halo_copies(n, channels):
         copies = []
         for i, (a, b) in enumerate(SIDES):
+            source = turned if b else own
             if a:
-                src = own.at[n, pl.ds(0, channels), (a + 1) // 2]
-                dst = arrive.at[n, i, pl.ds(0, channels), 0]
+                src = source.at[n, pl.ds(0, channels), pl.ds(12 if a > 0 else 0, 12)]
+                dst = arrive.at[n, i, pl.ds(0, channels), pl.ds(0, 12)]
             else:
-                src = own.at[n, pl.ds(0, channels)]
+                src = source.at[n, pl.ds(0, channels)]
                 dst = arrive.at[n, i, pl.ds(0, channels)]
             copies.append(
                 pltpu.make_async_remote_copy(
@@ -183,89 +232,68 @@
         pltpu.make_async_copy(grid.at[g], grid.at[g], all_send.at[g]).wait()
 
     def place(n, channel, target):
-        for ix in range(2):
-            start = PAD + 12 * (ix + 1) + 3
-            target[start : start + 6] = own[n, channel, ix, 0:6]
-        for i, (a, b) in enumerate(SIDES):
-            for ix in range(2) if a == 0 else (0,):
-                wx = ix + 1 if a == 0 else (0 if a == 1 else 3)
-                start = PAD + 12 * wx
-                if b == 0:
-                    target[start + 3 : start + 9] = arrive[n, i, channel, ix, 0:6]
-                elif b == 1:
-                    target[start : start + 3] = arrive[n, i, channel, ix, 3:6]
-                else:
-                    target[start + 9 : start + 12] = arrive[n, i, channel, ix, 0:3]
-
-    hz, cy, cx = lane8 % 8, lane8 // 8 % 4, lane8 // 32
-    target_odd = (hz % 2) == 0
-
-    def carried(cell, n):
-        if n % 2 == 0:
-            d = n // 2
-            return cell < d if d > 0 else cell >= 4 + d
-        low, high = (n - 1) // 2, (n + 1) // 2
-        if n > 0:
-            return (target_odd & (cell < high)) | (~target_odd & (cell < low))
-        return (target_odd & (cell >= 4 + high)) | (~target_odd & (cell >= 4 + low))
-
-    sign = lambda n: (n > 0) - (n < 0)
-    carry_x = {n: carried(cx, n) for n in (-3, -2, -1, 1, 2, 3)}
-    carry_y = {n: carried(cy, n) for n in (-3, -2, -1, 1, 2, 3)}
-    carry_z = {n: (hz < n if n > 0 else hz >= 8 + n) for n in (-3, -2, -1, 1, 2, 3)}
-
-    def combos(total):
-        found = []
-        for nx, ny, nz in OFFSETS[:total]:
-            if ny and (ny, nz) not in found:
-                found.append((ny, nz))
-        return found
-
-    slots = {c: i for i, c in enumerate(combos(len(OFFSETS)))}
-
-    def stages(total, k):
-        depths = sorted({nz for _, _, nz in OFFSETS[:total] if nz})
+        for start, size, a in ((0, 12, 1), (12, 24, 0), (36, 12, -1)):
+            low = arrive[n, SIDES.index((a, 1)), channel, 0:size]
+            high = arrive[n, SIDES.index((a, -1)), channel, 0:size]
+            middle = arrive[n, SIDES.index((a, 0)), channel, 0:size] if a else own[n, channel]
+            lane = lax.broadcasted_iota(jnp.int32, (size, TILE), 1)
+            target[PAD + start : PAD + start + size] = jnp.where(
+                lane < 32, low, jnp.where(lane < 96, middle, high)
+            )
+
+    carry = {n: (hz < n if n > 0 else hz >= 8 + n) for n in (-3, -2, -1, 1, 2, 3)}
+
+    def stage(total, k):
+        wanted = combos(total)
         for block in range(ROWS // 8):
             r = PAD + 8 * block
             t = (rows8 + 8 * block) % 3
             middle = win[k, r : r + 8]
             up = jnp.where(t < 2, win[k, r + 1 : r + 9], win[k, r - 2 : r + 6])
             down = jnp.where(t > 0, win[k, r - 1 : r + 7], win[k, r + 2 : r + 10])
-            for nz in depths:
-                zed[nz + 3, k, r : r + 8] = jnp.where(carry_z[nz], up if nz > 0 else down, middle)
-            zed[3, k, r : r + 8] = middle
-        for block in range(ROWS // 8):
-            r = PAD + 8 * block
-            for ny, nz in combos(total):
-                e = r + 3 * sign(ny)
-                wye[slots[ny, nz], k, r : r + 8] = jnp.where(
-                    carry_y[ny], zed[nz + 3, k, e : e + 8], zed[nz + 3, k, r : r + 8]
-                )
+            for depth in sorted({nz for _, nz in wanted}):
+                source = jnp.where(carry[depth], up if depth > 0 else down, middle) if depth else middle
+                for ny, nz in wanted:
+                    if nz == depth:
+                        i = SLOT[ny, nz]
+                        shifted[i, k, r : r + 8] = spread(source, lanes[SOURCE + i])
 
     def neighbour(o, k, r):
         nx, ny, nz = OFFSETS[o]
-        get = (lambda q: wye[slots[ny, nz], k, q : q + 8]) if ny else (lambda q: zed[nz + 3, k, q : q + 8])
-        here = get(r)
-        if nx:
-            here = jnp.where(carry_x[nx], get(r + 12 * sign(nx)), here)
-        return spread(here, lanes[o])
+        i = SLOT[ny, nz]
+        get = (lambda q: shifted[i, k, q : q + 8]) if (ny, nz) != (0, 0) else (lambda q: win[k, q : q + 8])
+        if nx % 2 == 0:
+            return get(r + 3 * (nx // 2))
+        return jnp.where(odd, get(r + 3 * ((nx + 1) // 2)), get(r + 3 * ((nx - 1) // 2)))
 
     def pair(o, r, mine):
-        nx, ny, nz = OFFSETS[o]
         delta = [
-            (mine[k] - (0.5 * EDGE) * n) - neighbour(o, k, r) for k, n in enumerate((nx, ny, nz))
+            (mine[k] - (0.5 * EDGE) * n) - neighbour(o, k, r) for k, n in enumerate(OFFSETS[o])
         ]
         square = delta[0] * delta[0] + delta[1] * delta[1] + delta[2] * delta[2]
         inverse = lax.rsqrt(square)
         return delta, square * inverse, inverse
 
+    def masks(first, last):
+        for block in range(BLOCKS):
+            start = FIRST + 8 * block
+            cell = (rows8 + start) // 3 % 4
+            known = live_win[PAD + start : PAD + start + 8]
+            over = {}
+            for nx in range(-3, 4):
+                dx = cell + (nx // 2 if nx % 2 == 0 else (nx - 1) // 2 + hz % 2)
+                over[nx] = jnp.where(dx > 3, 9, jnp.where(dx < 0, -9, 0))
+            for o in range(first, last):
+                nx, ny, nz = OFFSETS[o]
+                mask[o, 8 * block : 8 * block + 8] = spread(known, lanes[CODE + SLOT[ny, nz]] + over[nx])
+
     def step(n, total):
         for k in range(3):
             place(n, k, win.at[k])
         for k in range(3):
-            stages(total, k)
-        for block in range(ROWS // 8):
-            r = PAD + 8 * block
+            stage(total, k)
+        for block in range(BLOCKS):
+            r = PAD + FIRST + 8 * block
             mine = [win[k, r : r + 8] for k in range(3)]
             density = zero8
             for o in range(total):
@@ -273,11 +301,11 @@
                 gap = jnp.minimum(distance - RC, 0.0)
                 density = density + mask[o, 8 * block : 8 * block + 8] * (gap * gap)
             win[3, r : r + 8] = -EMBED * lax.rsqrt(density)
-        stages(total, 3)
+        stage(total, 3)
         forces = []
-        for ix in range(2):
-            q = 15 + 12 * ix
-            r = PAD + q
+        for block in range(OWN // 8):
+            r = PAD + 12 + 8 * block
+            q = 12 - FIRST + 8 * block
             mine = [win[k, r : r + 8] for k in range(3)]
             slope = win[3, r : r + 8]
             total_force = [zero8] * 3
@@ -307,29 +335,33 @@
 
     def advance(n, forces):
         column = jnp.broadcast_to(field[mx, pl.ds(my, 1), :], (8, TILE))
-        local = spread(column, planes[0])
-        push = jnp.sqrt((2.0 * MASS / DT) * local)
-        power = zero8
-        largest = zero8
-        for ix in range(2):
+        power, largest = [], zero8
+        for block in range(OWN // 8):
+            at = slice(8 * block, 8 * block + 8)
+            push = jnp.sqrt((2.0 * MASS / DT) * spread(column, lanes[PLANE + block]))
             reach = zero8
+            energy = zero8
             for k in range(3):
-                speed = vel[k, ix]
-                speed = speed + (DT / MASS) * (forces[ix][k] - MASS * speed + push * kick[n, k, ix])
-                vel[k, ix] = speed
-                moved = own[n, k, ix] + DT * speed
-                own[n + 1, k, ix] = moved
+                speed = vel[k, at]
+                speed = speed + (DT / MASS) * (forces[block][k] - MASS * speed + push * kick[n, k, at])
+                vel[k, at] = speed
+                moved = win[k, PAD + 12 + 8 * block : PAD + 20 + 8 * block] + DT * speed
+                own[n + 1, k, at] = moved
+                turned[n + 1, k, at] = pltpu.roll(moved, 64, 1)
                 reach = reach + moved * moved
-                power = power + jnp.where(inside, speed * speed, 0.0)
+                energy = energy + speed * speed
             largest = jnp.maximum(largest, reach)
-        return (MASS * DT) * power, largest
+            power.append(energy)
+        return power, largest
 
     def energies(n, power, largest):
-        power = power + pltpu.roll(power, 5, 0)
-        for shift in (8, 16, 32, 64):
-            power = power + pltpu.roll(power, shift, 1)
-        out = jnp.where(planes[2] > 0, spread(power, planes[1]), 0.0)
-        out = jnp.sum(out, axis=0, keepdims=True)
+        out = zero8
+        for block in range(OWN // 8):
+            value = power[block]
+            for shift in (8, 16, 32, 64):
+                value = value + pltpu.roll(value, shift, 1)
+            out = out + jnp.where(lanes[HELD + block] > 0, spread(value, lanes[BACK]), 0.0)
+        out = (MASS * DT) * jnp.sum(out, axis=0, keepdims=True)
         top = jnp.max(jnp.max(jnp.where(inside, largest, 0.0), axis=1, keepdims=True), axis=0, keepdims=True)
         row[n + 1, 0:1] = jnp.where(lane8[0:1] == 1, top, out)
 
@@ -355,73 +387,111 @@
         energies(n, power, largest)
         send_all(n + 1)
 
+        @pl.when(n == 0)
+        def _():
+            masks(NEAR, len(OFFSETS))
+
         @pl.when(n < STEPS - 1)
         def _():
-            for c in halo_copies(n + 1, 3):
+            waits = halo_copies(n + 1, 3)
+            for c in waits:
                 c.wait_recv()
-            for c in halo_copies(n + 1, 3):
+            for c in waits:
                 c.wait_send()
 
-    for c in halo_copies(0, 4):
+    first = halo_copies(0, 4)
+    for c in first:
         c.start()
     send_all(0)
-    for c in halo_copies(0, 4):
+    for n in range(STEPS):
+        for k in range(3):
+            unpack(6 + 3 * n + k, kick.at[n, k])
+    for c in first:
         c.wait_recv()
-    for c in halo_copies(0, 4):
+    for c in first:
         c.wait_send()
 
     place(0, 3, live_win)
-    for block in range(ROWS // 8):
-        known = live_win[PAD + 8 * block : PAD + 8 * block + 8]
-        for o in range(len(OFFSETS)):
-            mask[o, 8 * block : 8 * block + 8] = spread(known, lanes[len(OFFSETS) + o])
+    masks(0, NEAR)
 
     lax.fori_loop(0, 2, lambda n, c: (full_step(n, NEAR), c)[1], 0)
     lax.fori_loop(2, 4, lambda n, c: (full_step(n, len(OFFSETS)), c)[1], 0)
 
-    for k in range(3):
-        for ix in range(2):
-            for iy in range(2):
-                u_out[k, ix, iy] = own[STEPS, k, ix, 3 * iy : 3 * iy + 3]
-                v_out[k, ix, iy] = vel[k, ix, 3 * iy : 3 * iy + 3]
+    for c in range(6):
+        held = own.at[STEPS, c] if c < 3 else vel.at[c - 3]
+        for cell in range(4):
+            for ix in range(2):
+                start = (4 * ix + cell) * 3
+                raw[0, cell, 3 * ix : 3 * ix + 3] = held[start : start + 3]
+        for iy in range(2):
+            value = zero8
+            for cell in range(4):
+                part = raw[0, cell]
+                part = part if cell == 1 + iy else pltpu.roll(part, (32 * (cell - 1 - iy)) % TILE, 1)
+                value = jnp.where(lane8 // 32 == cell, part, value)
+            back[iy, c] = value
+    stores = []
+    for ix in range(2):
+        for iy in range(2):
+            spot = pl.ds(3 * ix, 3)
+            at = 3 + 3 * (2 * ix + iy)
+            stores += [
+                pltpu.make_async_copy(back.at[iy, pl.ds(0, 3), spot], u_out.at[:, ix, :, iy], in_sem.at[at]),
+                pltpu.make_async_copy(back.at[iy, pl.ds(3, 3), spot], v_out.at[:, ix, :, iy], in_sem.at[at + 1]),
+            ]
+    for copy in stores:
+        copy.start()
+    lane1 = lane8[0:1] == 1
     near = jnp.max(jnp.max(grid[1], axis=0), axis=0, keepdims=True)
     far = jnp.maximum(jnp.max(grid[2], axis=0), jnp.max(grid[3], axis=0))
     far = jnp.max(far, axis=0, keepdims=True)
-    flag_out[...] = jnp.where((near <= NEAR_LIMIT) & (far <= FAR_LIMIT), 1.0, 0.0)
+    fine = jnp.where((near <= NEAR_LIMIT) & (far <= FAR_LIMIT), 1.0, 0.0)
+    flag_out[0, 0] = jnp.sum(jnp.where(lane1, fine, 0.0))
 
     wait_all(STEPS)
     deposit(STEPS)
     lane3 = lax.broadcasted_iota(jnp.int32, (NGX, NGY, TILE), 2)
     heat_out[0] = jnp.sum(jnp.where(lane3 == mx * NGY + my, field[...], 0.0), axis=2)
+    for copy in stores:
+        copy.wait()
 
 
 def fast(displacement, velocity, noise, electron_temp, pair_list, pair_count):
-    block = (3, 2, 2, TZ, TILE)
-    whole = pl.BlockSpec(memory_space=pltpu.VMEM)
+    turn = lambda v: jnp.swapaxes(v, -3, -2)
+    brick = (3, 2, TZ, 2, TILE)
+    hbm = pl.BlockSpec(memory_space=pltpu.HBM)
+    vmem = pl.BlockSpec(memory_space=pltpu.VMEM)
     total = len(OFFSETS)
-    return pl.pallas_call(
+    tables = lane_tables()
+    u, v, heat, flag = pl.pallas_call(
         body,
         out_shape=(
-            jax.ShapeDtypeStruct(block, F32),
-            jax.ShapeDtypeStruct(block, F32),
+            jax.ShapeDtypeStruct(brick, F32),
+            jax.ShapeDtypeStruct(brick, F32),
             jax.ShapeDtypeStruct((1, NGX, NGY), F32),
-            jax.ShapeDtypeStruct((1, TILE), F32),
+            jax.ShapeDtypeStruct((1, 1), F32),
         ),
-        in_specs=[whole] * 8,
-        out_specs=(whole,) * 4,
+        in_specs=[hbm] * 5 + [vmem, hbm],
+        out_specs=(hbm, hbm, vmem, pl.BlockSpec(memory_space=pltpu.SMEM)),
         scratch_shapes=[
-            pltpu.VMEM((STEPS + 1, 4, 2, 8, TILE), F32),
-            pltpu.VMEM((STEPS, 8, 4, 2, 8, TILE), F32),
+            pltpu.VMEM((STEPS + 1, 4, OWN, TILE), F32),
+            pltpu.VMEM((STEPS + 1, 4, OWN, TILE), F32),
+            pltpu.VMEM((STEPS, 8, 4, OWN, TILE), F32),
             pltpu.VMEM((STEPS + 1, NGX, NGY, TILE), F32),
             pltpu.VMEM((STEPS + 1, 8, TILE), F32),
             pltpu.VMEM((4, FLAT, TILE), F32),
-            pltpu.VMEM((7, 4, FLAT, TILE), F32),
-            pltpu.VMEM((18, 4, FLAT, TILE), F32),
-            pltpu.VMEM((total, ROWS, TILE), F32),
+            pltpu.VMEM((len(SHIFTS), 4, FLAT, TILE), F32),
+            pltpu.VMEM((total, 8 * BLOCKS, TILE), F32),
             pltpu.VMEM((FLAT, TILE), F32),
-            pltpu.VMEM((3, 2, 8, TILE), F32),
-            pltpu.VMEM((STEPS, 3, 2, 8, TILE), F32),
+            pltpu.VMEM((3, OWN, TILE), F32),
+            pltpu.VMEM((STEPS, 3, OWN, TILE), F32),
             pltpu.VMEM((NGX, NGY, TILE), F32),
+            pltpu.VMEM((2, 18, 8, TILE), F32),
+            pltpu.VMEM((2, 6, 8, TILE), F32),
+            pltpu.VMEM((1, NGX, NGY), F32),
+            pltpu.VMEM((1, 1, 2, PAIRS), jnp.int32),
+            pltpu.VMEM(tables.shape, jnp.int32),
+            pltpu.SemaphoreType.DMA((15 + 4 * STEPS,)),
             pltpu.SemaphoreType.DMA((STEPS, 8)),
             pltpu.SemaphoreType.DMA((STEPS, 8)),
             pltpu.SemaphoreType.DMA((STEPS + 1,)),
@@ -431,10 +501,8 @@
         compiler_params=pltpu.CompilerParams(
             collective_id=0, has_side_effects=True, vmem_limit_bytes=40 << 20
         ),
-    )(
-        displacement, velocity, noise, electron_temp, pair_list, pair_count,
-        jnp.asarray(lane_tables()), jnp.asarray(plane_tables()),
-    )
+    )(turn(displacement), turn(velocity), turn(noise), electron_temp, pair_list, pair_count, jnp.asarray(tables))
+    return turn(u), turn(v), heat, flag
 
 
 def padded_2(values, sides, width):
@@ -539,7 +607,7 @@
 
 def per_device(*arguments):
     *results, flag = fast(*arguments)
-    return lax.cond(flag[0, 1] > 0.5, lambda: tuple(results), lambda: slow(*arguments))
+    return lax.cond(flag[0, 0] > 0.5, lambda: tuple(results), lambda: slow(*arguments))
 
 
 def solution(mesh):

time: 58.3 us -> 55.1 us (0.945)
  local copies, waits for them, and re-layouts: 5.22 us -> 3.6 us
  Pallas kernels: 50.5 us -> 49.1 us
    pallas_call x1, Pallas kernels: 50.5 us -> 49.1 us  [fast(): pl.pallas_call(body, out_shape=(jax.ShapeDtypeStruct(brick, F32), jax.Sha...]
    cond x3 -> x1, local copies, waits for them, and re-layouts: 1.23 us -> 0.01 us  [the longest x2 1.23 us: per_device(): lax.cond(flag[0, 1] > 0.5, lambda: tuple(results), lambda: slow(*arguments))]
    unnamed x16 -> x13, local copies, waits for them, and re-layouts: 3.38 us -> 3.6 us
where the time goes in v2:
time: 55.1 us; the launch traced here: 54.8 us
  Pallas kernels  49.1 us (89%)
  local copies, waits for them, and re-layouts  3.6 us (7%)
  between operations  1.96 us (4%)
    pallas_call x1, Pallas kernels, fast(): pl.pallas_call(body, out_shape=(jax.ShapeDtypeStruct(brick, F32), jax.Sha...  49.1 us
    unnamed x13, local copies, waits for them, and re-layouts  3.6 us

profile of v2, /device:TPU:1, one launch (start us, length us, event | category | flops | bytes accessed | tf_op | source)
XLA Modules:
  0.0 54.8 jit_solution(3734928335384326722)
XLA Ops:
  0.6 0.7 %copy.151.heat_in = f32[1,8,16]{2,1,0:T(8,128)S(1)} copy(f32[1,8,16]{2,1,0:T(8,128)} %param.21) | data formatting | bytes 1024
  2.0 0.0 copy-start.3
  2.0 0.7 %copy-done.3 = s32[1,1,2,324]{3,2,1,0:T(2,128)S(1)} copy-done((s32[1,1,2,324]{3,2,1,0:T(2,128)S(1)}, s32[1,1,2,324]{3,2,1,0:T(2,128)}, u32[]{:S(2)}) %copy-start.3) | copy-done | bytes 2616
  2.7 0.0 copy-start
  2.7 0.9 %copy-done = s32[48,8,128]{2,1,0:T(8,128)S(1)} copy-done((s32[48,8,128]{2,1,0:T(8,128)S(1)}, s32[48,8,128]{2,1,0:T(8,128)}, u32[]{:S(2)}) %copy-start) | copy-done | bytes 196632
  3.6 0.0 copy-start.5
  3.6 49.1 %shard_map.104 = (f32[3,2,3,2,128]{4,3,2,1,0:T(2,128)S(1)}, f32[3,2,3,2,128]{4,3,2,1,0:T(2,128)S(1)}, f32[1,8,16]{2,1,0:T(8,128)S(1)}, f32[1,1]{1,0:T(1,128)}) custom-call(f32[3,2,3,2,128]{4,3,2,1,0:T(2,128)} %bitcast.154, f32[3,2,3,2,128]{4,3,2,1,0:T(2,128)} %bitcast.155, f32[4,3,2,3,2,128]{5,4,3,2,1,0:T(2,128)} %bitcast.152, ...), custom_call_target="tpu_custom_call" | custom-call | tf_op jit(solution)/shard_map/pallas_call | solution.py:466
  52.7 0.0 copy-start.4
  53.4 0.0 copy-done.5
  53.4 0.1 copy-done.4
  53.4 0.1 conditional.1
  53.6 0.0 copy-start.1
  53.6 0.6 %copy.153 = f32[3,2,2,3,128]{4,2,3,1,0:T(2,128)} copy(f32[3,2,2,3,128]{4,2,3,1,0:T(2,128)S(1)} %get-tuple-element.1787) | data formatting | bytes 36864
  54.2 0.0 copy-done.1
  54.2 0.6 %copy.154 = f32[3,2,2,3,128]{4,2,3,1,0:T(2,128)} copy(f32[3,2,2,3,128]{4,2,3,1,0:T(2,128)S(1)} %get-tuple-element.1788) | data formatting | bytes 36864
  (1 shorter events, 0.0 us)
Async XLA Ops:
  2.0 0.7 %copy-start.3 = (s32[1,1,2,324]{3,2,1,0:T(2,128)S(1)}, s32[1,1,2,324]{3,2,1,0:T(2,128)}, u32[]{:S(2)}) copy-start(s32[1,1,2,324]{3,2,1,0:T(2,128)} %pairs_in.1) | copy-start | bytes 7780
  2.7 0.9 %copy-start = (s32[48,8,128]{2,1,0:T(8,128)S(1)}, s32[48,8,128]{2,1,0:T(8,128)}, u32[]{:S(2)}) copy-start(s32[48,8,128]{2,1,0:T(8,128)} %constant.771.clone.tables) | copy-start | bytes 589828
  3.6 49.8 %copy-start.5 = (f32[3,2,2,3,128]{4,2,3,1,0:T(2,128)S(1)}, f32[3,2,2,3,128]{4,2,3,1,0:T(2,128)}, u32[]{:S(2)}) copy-start(f32[3,2,2,3,128]{4,2,3,1,0:T(2,128)} %param.19) | copy-start | bytes 55300
  52.7 0.7 %copy-start.4 = (f32[3,2,2,3,128]{4,2,3,1,0:T(2,128)S(1)}, f32[3,2,2,3,128]{4,2,3,1,0:T(2,128)}, u32[]{:S(2)}) copy-start(f32[3,2,2,3,128]{4,2,3,1,0:T(2,128)} %param.18) | copy-start | bytes 55300
  53.6 0.6 %copy-start.1 = (f32[1,8,16]{2,1,0:T(8,128)}, f32[1,8,16]{2,1,0:T(8,128)S(1)}, u32[]{:S(2)}) copy-start(f32[1,8,16]{2,1,0:T(8,128)S(1)} %get-tuple-element.1789) | copy-start | bytes 1540

commit v3 on v2

--- a/solution.py
+++ b/solution.py
@@ -1,3 +1,4 @@
+import math
 from functools import partial
 
 import jax
@@ -57,39 +58,55 @@
 SLOT = {c: i for i, c in enumerate(SHIFTS)}
 SLOT[0, 0] = len(SHIFTS)
 SIDES = [(a, b) for a in (-1, 0, 1) for b in (-1, 0, 1) if (a, b) != (0, 0)]
-HOPS = sorted(
-    (
-        (dx, dy, dz, dc)
-        for dx in range(4)
-        for dy in range(4)
-        for dz in range(4)
-        for dc in range(2)
-        if (dx, dy, dz, dc) != (0, 0, 0, 0)
-    ),
-    key=lambda d: -sum(min(v, 4 - v) for v in d[:3]) * 2 - d[3],
+SOURCE, CODE, PLANE, BACK, HELD = 0, 20, 41, 44, 45
+TABLES = 48
+
+
+def ring(d, n):
+    return min(d % n, -d % n)
+
+
+def hops(a, b):
+    most = 0
+    for mx in range(NGX):
+        for my in range(NGY):
+            px, py = (mx + a) % NGX, (my + b) % NGY
+            rows = ring(px - mx, 4) + ring(py // 4 - my // 4, 4)
+            depth = (py // 2 % 2 - my // 2 % 2) * 2 + px // 4 - mx // 4
+            most = max(most, rows + ring(depth, 4))
+    return most
+
+
+def is_near(a, b):
+    return ring(a, NGX) + ring(b, NGY) <= SUB
+
+
+PEERS = sorted(
+    ((a, b) for a in range(NGX) for b in range(NGY) if (a, b) != (0, 0)),
+    key=lambda p: -hops(*p) + (0 if is_near(*p) else 1.5),
 )
-SOURCE, CODE, PLANE, BACK, HELD = 0, 20, 41, 44, 45
-
-
-def lane_tables():
-    s = np.arange(TILE)
-    cell, hz = s // 8, s % 8
-    out = []
-    for ny, nz in SHIFTS:
-        dy = (ny - ny % 2) // 2 + ny % 2 * (hz % 2)
-        out.append((cell + dy) % 16 * 8 + (hz + nz) % 8)
-    for ny, nz in SHIFTS + [(0, 0)]:
-        dy = (ny - ny % 2) // 2 + ny % 2 * (hz % 2)
-        out.append(s // 32 * 32 + 9 + 3 * ((cell % 4 + dy) // 4 + 1) + (hz + nz) // 8 + 1)
-    out = [np.broadcast_to(v[None, :], (8, TILE)) for v in out]
-    rows = np.arange(OWN)[:, None] % 3
-    out += list(((rows * 8 + hz[None, :]) * 128 // 24).reshape(3, 8, TILE))
-    back, held = np.zeros((8, TILE)), np.zeros((OWN, TILE))
-    for layer in range(24):
-        back[:, layer * 128 // 24] = layer % 8
-        held[:, layer * 128 // 24] = rows[:, 0] == layer // 8
-    out += [back] + list(held.reshape(3, 8, TILE))
-    return np.stack(out).astype(np.int32)
+NEAR_ROWS = 1 + sum(is_near(*p) for p in PEERS)
+FAR_ROWS = NGX * NGY - NEAR_ROWS
+
+
+def column_weights():
+    keep, powers = np.zeros((NGX, NGY)), []
+    keep[0, 0] = 1.0
+    for _ in range(SUB + 1):
+        powers.append(keep)
+        beside = sum(np.roll(keep, d, axis) for axis in (0, 1) for d in (1, -1))
+        keep = (1 - 6 * RATE) * keep + RATE * beside
+    return [
+        sum(math.comb(SUB, c) * math.comb(c, (c - d) // 2) * RATE**c * powers[SUB - c] for c in range(d, SUB + 1, 2))
+        for d in range(SUB + 1)
+    ]
+
+
+WEIGHTS = column_weights()
+TERMS = [
+    (c, a, h) for c in range(SUB + 1) for a in range(NGX) for h in range(2)
+    if np.any(WEIGHTS[c][a, 8 * h : 8 * h + 8] != 0)
+]
 
 
 def spread(x, index):
@@ -97,27 +114,18 @@
 
 
 def body(
-    u_in, v_in, noise, heat_in, pairs_in, count, tables,
-    u_out, v_out, heat_out, flag_out,
-    own, turned, arrive, grid, row, win, shifted, mask, live_win, vel, kick, field,
-    raw, back, heat, pairs, lanes,
-    in_sem, halo_send, halo_recv, all_send, all_recv, junk,
+    u_in, v_in, noise, heat_in, pairs_in, count,
+    u_out, v_out, heat_out, flag_out, heat_same, pairs_same,
+    own, packed, arrive_x, arrive_y, top, grid, grid_turned, near, far, weigh, column, row, win, shifted, mask, live_win, vel, kick, field,
+    raw, back, heat, pairs, live_count, lanes,
+    in_sem, halo_send, halo_recv, all_send, all_recv, far_recv, junk,
 ):
     mx, my = lax.axis_index("gx"), lax.axis_index("gy")
-    x, zl = lax.rem(mx, 4), mx // 4
-    y, zh, core = my // 4, lax.rem(my // 2, 2), lax.rem(my, 2)
-    z = zh * 2 + zl
-    xs = [lax.rem(x + d, 4) for d in range(4)]
-    ys = [lax.rem(y + d, 4) for d in range(4)]
-    zs = [lax.rem(z + d, 4) for d in range(4)]
-    cs = [lax.rem(core + d, 2) for d in range(2)]
-    gxs = {(dx, dz): lax.rem(zs[dz], 2) * 4 + xs[dx] for dx in range(4) for dz in range(4)}
-    gys = {
-        (dy, dz, dc): ys[dy] * 4 + zs[dz] // 2 * 2 + cs[dc]
-        for dy in range(4) for dz in range(4) for dc in range(2)
-    }
-    peers = [(gxs[dx, dz], gys[dy, dz, dc]) for dx, dy, dz, dc in HOPS]
-    sides = [(lax.rem(mx + a + NGX, NGX), lax.rem(my + b + NGY, NGY)) for a, b in SIDES]
+    gxs = [lax.rem(mx + d, NGX) for d in range(NGX)]
+    gys = [lax.rem(my + d, NGY) for d in range(NGY)]
+    gxs_back = [lax.rem(NGX + d - mx, NGX) for d in range(NGX)]
+    peers = [(gxs[a], gys[b]) for a, b in PEERS]
+    sides = [(gxs[a % NGX], gys[b % NGY]) for a, b in SIDES]
 
     barrier = pltpu.get_barrier_semaphore()
     for peer in peers:
@@ -126,7 +134,7 @@
     loads = [
         pltpu.make_async_copy(pairs_in, pairs, in_sem.at[0]),
         pltpu.make_async_copy(heat_in, heat, in_sem.at[1]),
-        pltpu.make_async_copy(tables, lanes, in_sem.at[2]),
+        pltpu.make_async_copy(count, live_count, in_sem.at[2]),
     ]
     for ix in range(2):
         for iy in range(2):
@@ -159,6 +167,26 @@
             shifted[i, k, 0:PAD] = jnp.zeros((PAD, TILE), F32)
             shifted[i, k, PAD + ROWS : FLAT] = jnp.zeros((PAD, TILE), F32)
 
+    cell = lane8 // 8
+    for i, (ny, nz) in enumerate(SHIFTS + [(0, 0)]):
+        dy = (ny - ny % 2) // 2 + (hz % 2 if ny % 2 else 0)
+        if i < len(SHIFTS):
+            lanes[SOURCE + i] = (cell + dy + 16) % 16 * 8 + (hz + nz + 8) % 8
+        above = (cell % 4 + dy + 4) // 4 - 1
+        lanes[CODE + i] = lane8 // 32 * 32 + 9 + 3 * (above + 1) + (hz + nz + 8) // 8
+    layer = (3 * lane8 + 15) // 16
+    lanes[BACK] = layer % 8
+    for i in range(OWN // 8):
+        t = (rows8 + 8 * i) % 3
+        lanes[PLANE + i] = (t * 8 + hz) * 16 // 3
+        lanes[HELD + i] = jnp.where((layer * 16 // 3 == lane8) & (layer // 8 == t), 1, 0)
+    for i, (c, a, h) in enumerate(TERMS):
+        value = zero8
+        for j in range(8):
+            if WEIGHTS[c][a, 8 * h + j]:
+                value = jnp.where(rows8 == j, float(WEIGHTS[c][a, 8 * h + j]), value)
+        weigh[i] = value
+
     for copy in loads:
         copy.wait()
 
@@ -179,11 +207,21 @@
         unpack(k, own.at[0, k])
         unpack(3 + k, vel.at[k])
 
+    def pack(n, values, start, size):
+        group = lax.broadcasted_iota(jnp.int32, (size, TILE), 1) // 32
+        for half in range(2):
+            out = None
+            for k, value in enumerate(values):
+                turn = (32 * (k - 1 - half)) % TILE
+                value = pltpu.roll(value, turn, 1) if turn else value
+                out = value if out is None else jnp.where(group == k, value, out)
+            packed[n, half, start : start + size] = out
+
     p_row = lax.broadcasted_iota(jnp.int32, (OWN, PAIRS), 0)
     p_lane = lax.broadcasted_iota(jnp.int32, (TILE, PAIRS), 0)
     slot = lax.broadcasted_iota(jnp.int32, (OWN, PAIRS), 1)
-    tile, code = pairs[0, 0, 0:1, :], pairs[0, 0, 1:2, :]
-    named = (tile // 6 * 3 + tile % 3 == p_row // 12 * 3 + p_row % 3) & (slot < count[0:1, 0:1])
+    tile, code = pairs[0:1, :], pairs[1:2, :]
+    named = (tile // 6 * 3 + tile % 3 == p_row // 12 * 3 + p_row % 3) & (slot < live_count[0, 0])
     coded = tile // 3 % 2 * 32 + 32 + code == p_lane
     own[0, 3] = lax.dot_general(
         jnp.where(named, 1.0, 0.0).astype(jnp.bfloat16),
@@ -191,23 +229,23 @@
         (((1,), (1,)), ((), ())),
         preferred_element_type=F32,
     )
-    for k in range(4):
-        turned[0, k] = pltpu.roll(own[0, k], 64, 1)
+    pack(0, [own[0, k] for k in range(4)], 0, OWN)
+    top[...] = zero8
     for i in range(NGX):
-        row[0, 0:1, NGY * i : NGY * (i + 1)] = heat[0, i : i + 1, :]
+        row[0, 0:1, NGY * i : NGY * (i + 1)] = heat[i : i + 1, :]
 
     pl.semaphore_wait(barrier, len(peers))
 
     def halo_copies(n, channels):
         copies = []
         for i, (a, b) in enumerate(SIDES):
-            source = turned if b else own
-            if a:
-                src = source.at[n, pl.ds(0, channels), pl.ds(12 if a > 0 else 0, 12)]
-                dst = arrive.at[n, i, pl.ds(0, channels), pl.ds(0, 12)]
+            part = pl.ds(12 if a > 0 else 0, 12) if a else pl.ds(0, OWN)
+            if b:
+                src = packed.at[n, (b + 1) // 2, part]
+                dst = arrive_y.at[n, i, pl.ds(0, 12 if a else OWN)]
             else:
-                src = source.at[n, pl.ds(0, channels)]
-                dst = arrive.at[n, i, pl.ds(0, channels)]
+                src = own.at[n, pl.ds(0, channels), part]
+                dst = arrive_x.at[n, (a + 1) // 2, pl.ds(0, channels)]
             copies.append(
                 pltpu.make_async_remote_copy(
                     src_ref=src, dst_ref=dst, send_sem=halo_send.at[n, i], recv_sem=halo_recv.at[n, i],
@@ -216,26 +254,34 @@
             )
         return copies
 
-    def send_all(g):
+    def send_all(g, first):
         src = row.at[g, pl.ds(0, 1)]
-        dst = grid.at[g, mx, pl.ds(my, 1)]
-        for peer in peers:
+        for (a, b), peer in zip(PEERS, peers):
+            if first:
+                dst, done = grid.at[mx, pl.ds(my, 1)], all_recv.at[0]
+            else:
+                there = (-a % NGX, pl.ds(-b % NGY, 1))
+                dst = (near if is_near(a, b) else far).at[(g, *there)]
+                done = (all_recv if is_near(a, b) else far_recv).at[g]
             pltpu.make_async_remote_copy(
-                src_ref=src, dst_ref=dst, send_sem=all_send.at[g], recv_sem=all_recv.at[g],
+                src_ref=src, dst_ref=dst, send_sem=all_send.at[g], recv_sem=done,
                 device_id=peer, device_id_type=MESH,
             ).start()
-        pltpu.make_async_copy(src, dst, all_recv.at[g]).start()
-        pltpu.make_async_copy(src, junk.at[pl.ds(0, 1)], all_send.at[g]).start()
-
-    def wait_all(g):
-        pltpu.make_async_copy(grid.at[g], grid.at[g], all_recv.at[g]).wait()
-        pltpu.make_async_copy(grid.at[g], grid.at[g], all_send.at[g]).wait()
+        mine = grid.at[mx, pl.ds(my, 1)] if first else near.at[g, 0, pl.ds(0, 1)]
+        pltpu.make_async_copy(src, mine, all_recv.at[g]).start()
+        pltpu.make_async_copy(src, junk.at[pl.ds(g, 1)], all_send.at[g]).start()
+
+    def wait_rows(sem, count):
+        part = junk.at[pl.ds(0, count)]
+        pltpu.make_async_copy(part, part, sem).wait()
 
     def place(n, channel, target):
         for start, size, a in ((0, 12, 1), (12, 24, 0), (36, 12, -1)):
-            low = arrive[n, SIDES.index((a, 1)), channel, 0:size]
-            high = arrive[n, SIDES.index((a, -1)), channel, 0:size]
-            middle = arrive[n, SIDES.index((a, 0)), channel, 0:size] if a else own[n, channel]
+            low = arrive_y[n, SIDES.index((a, 1)), 0:size]
+            high = arrive_y[n, SIDES.index((a, -1)), 0:size]
+            low = pltpu.roll(low, TILE - 32 * channel, 1) if channel else low
+            high = pltpu.roll(high, 96 - 32 * channel, 1) if channel < 3 else high
+            middle = arrive_x[n, (a + 1) // 2, channel] if a else own[n, channel]
             lane = lax.broadcasted_iota(jnp.int32, (size, TILE), 1)
             target[PAD + start : PAD + start + size] = jnp.where(
                 lane < 32, low, jnp.where(lane < 96, middle, high)
@@ -328,68 +374,116 @@
             t = t + RATE * (beside - 6.0 * t)
         return t
 
+    def near_part(g, a, h, other):
+        most = SUB - ring(a, NGX)
+        within = rows8 <= most if h == 0 else rows8 >= 8 - most
+        return jnp.where(within, near[g, a, 8 * h : 8 * h + 8], other)
+
+    def weighed(get, marked):
+        sums = [zero8] * (SUB + 1)
+        for i, (c, a, h) in enumerate(TERMS):
+            sums[c] = sums[c] + weigh[i] * get(a, h)
+        if marked:
+            sums = [jnp.where(lane8 == 1, 0.0, v) for v in sums]
+        total = sums[0]
+        for d in range(1, SUB + 1):
+            total = total + (pltpu.roll(sums[d], d, 1) + pltpu.roll(sums[d], TILE - d, 1))
+        return total
+
+    def field_rows(a, h):
+        return field[a, 8 * h : 8 * h + 8]
+
+    def gathered_rows(g):
+        return jnp.stack([
+            jnp.concatenate([near_part(g, a, h, far[g, a, 8 * h : 8 * h + 8]) for h in range(2)], axis=0)
+            for a in range(NGX)
+        ])
+
     def deposit(g):
         lane3 = lax.broadcasted_iota(jnp.int32, (NGX, NGY, TILE), 2)
-        added = jnp.where(lane3 == 1, 0.0, grid[g]) * (1.0 / HEAT)
-        field[...] = diffuse(field[...] + added)
+        added = jnp.where(lane3 == 1, 0.0, gathered_rows(g)) * (1.0 / HEAT)
+        return diffuse(field[...] + added)
 
     def advance(n, forces):
-        column = jnp.broadcast_to(field[mx, pl.ds(my, 1), :], (8, TILE))
-        power, largest = [], zero8
+        local = jnp.broadcast_to(jnp.sum(column[...], axis=0, keepdims=True), (8, TILE))
+        power = []
         for block in range(OWN // 8):
             at = slice(8 * block, 8 * block + 8)
-            push = jnp.sqrt((2.0 * MASS / DT) * spread(column, lanes[PLANE + block]))
-            reach = zero8
-            energy = zero8
+            push = jnp.sqrt((2.0 * MASS / DT) * spread(local, lanes[PLANE + block]))
+            energy, places = zero8, []
             for k in range(3):
                 speed = vel[k, at]
                 speed = speed + (DT / MASS) * (forces[block][k] - MASS * speed + push * kick[n, k, at])
                 vel[k, at] = speed
                 moved = win[k, PAD + 12 + 8 * block : PAD + 20 + 8 * block] + DT * speed
                 own[n + 1, k, at] = moved
-                turned[n + 1, k, at] = pltpu.roll(moved, 64, 1)
-                reach = reach + moved * moved
+                places.append(moved)
                 energy = energy + speed * speed
-            largest = jnp.maximum(largest, reach)
+            pack(n + 1, places, 8 * block, 8)
             power.append(energy)
-        return power, largest
-
-    def energies(n, power, largest):
+        return power
+
+    def energies(n, power):
         out = zero8
+        index = [lanes[BACK] + (32 + 8 * i) for i in range(8)]
         for block in range(OWN // 8):
-            value = power[block]
-            for shift in (8, 16, 32, 64):
-                value = value + pltpu.roll(value, shift, 1)
-            out = out + jnp.where(lanes[HELD + block] > 0, spread(value, lanes[BACK]), 0.0)
+            parts = [spread(power[block], i) for i in index]
+            while len(parts) > 1:
+                parts = [a + b for a, b in zip(parts[::2], parts[1::2])]
+            out = out + jnp.where(lanes[HELD + block] > 0, parts[0], 0.0)
         out = (MASS * DT) * jnp.sum(out, axis=0, keepdims=True)
-        top = jnp.max(jnp.max(jnp.where(inside, largest, 0.0), axis=1, keepdims=True), axis=0, keepdims=True)
-        row[n + 1, 0:1] = jnp.where(lane8[0:1] == 1, top, out)
+        row[n + 1, 0:1] = jnp.where(lane8[0:1] == 1, top[0:1], out)
+
+    def reach(n):
+        most = zero8
+        for block in range(OWN // 8):
+            at = slice(8 * block, 8 * block + 8)
+            square = sum(own[n + 1, k, at] * own[n + 1, k, at] for k in range(3))
+            most = jnp.maximum(most, jnp.where(inside, square, 0.0))
+        most = jnp.max(jnp.max(most, axis=1, keepdims=True), axis=0, keepdims=True)
+        top[...] = jnp.broadcast_to(most, (8, TILE))
 
     def full_step(n, total):
         forces = step(n, total)
-        wait_all(n)
 
         @pl.when(n == 0)
         def _():
-            field[...] = jnp.transpose(grid[0].reshape(TILE, TILE)).reshape(NGX, NGY, TILE)
+            wait_rows(all_recv.at[0], NGX * NGY)
+            turn = jnp.transpose(grid[...].reshape(TILE, TILE)).reshape(NGX, NGY, TILE)
+            grid_turned[...] = turn
+            column[0:1] = grid_turned[mx, pl.ds(my, 1), :]
+            column[1:8] = jnp.zeros((7, TILE), F32)
 
         @pl.when(n > 0)
         def _():
-            deposit(n)
-
-        power, largest = advance(n, forces)
+            wait_rows(all_recv.at[n], NEAR_ROWS)
+            arrived = weighed(lambda a, h: near_part(n, a, h, 0.0), True)
+            column[...] = column[...] + (1.0 / HEAT) * arrived
+
+        power = advance(n, forces)
 
         @pl.when(n < STEPS - 1)
         def _():
             for c in halo_copies(n + 1, 3):
                 c.start()
 
-        energies(n, power, largest)
-        send_all(n + 1)
-
+        energies(n, power)
+        send_all(n + 1, False)
+
+        reach(n)
         @pl.when(n == 0)
         def _():
             masks(NEAR, len(OFFSETS))
+            for a in range(NGX):
+                field[a] = pltpu.roll(grid_turned[gxs[a]], lax.rem(NGY - my, NGY), 0)
+
+        @pl.when(n > 0)
+        def _():
+            wait_rows(far_recv.at[n], FAR_ROWS)
+            field[...] = deposit(n)
+
+        column[...] = weighed(field_rows, False)
+        wait_rows(all_send.at[n], NGX * NGY)
 
         @pl.when(n < STEPS - 1)
         def _():
@@ -402,7 +496,7 @@
     first = halo_copies(0, 4)
     for c in first:
         c.start()
-    send_all(0)
+    send_all(0, True)
     for n in range(STEPS):
         for k in range(3):
             unpack(6 + 3 * n + k, kick.at[n, k])
@@ -430,7 +524,10 @@
                 part = part if cell == 1 + iy else pltpu.roll(part, (32 * (cell - 1 - iy)) % TILE, 1)
                 value = jnp.where(lane8 // 32 == cell, part, value)
             back[iy, c] = value
-    stores = []
+    stores = [
+        pltpu.make_async_copy(heat, heat_same, in_sem.at[1]),
+        pltpu.make_async_copy(pairs, pairs_same, in_sem.at[0]),
+    ]
     for ix in range(2):
         for iy in range(2):
             spot = pl.ds(3 * ix, 3)
@@ -442,16 +539,17 @@
     for copy in stores:
         copy.start()
     lane1 = lane8[0:1] == 1
-    near = jnp.max(jnp.max(grid[1], axis=0), axis=0, keepdims=True)
-    far = jnp.maximum(jnp.max(grid[2], axis=0), jnp.max(grid[3], axis=0))
-    far = jnp.max(far, axis=0, keepdims=True)
-    fine = jnp.where((near <= NEAR_LIMIT) & (far <= FAR_LIMIT), 1.0, 0.0)
-    flag_out[0, 0] = jnp.sum(jnp.where(lane1, fine, 0.0))
-
-    wait_all(STEPS)
-    deposit(STEPS)
-    lane3 = lax.broadcasted_iota(jnp.int32, (NGX, NGY, TILE), 2)
-    heat_out[0] = jnp.sum(jnp.where(lane3 == mx * NGY + my, field[...], 0.0), axis=2)
+    wait_rows(all_recv.at[STEPS], NEAR_ROWS)
+    wait_rows(far_recv.at[STEPS], FAR_ROWS)
+    wait_rows(all_send.at[STEPS], NGX * NGY)
+    most = [jnp.max(gathered_rows(g), axis=0) for g in range(2, STEPS + 1)]
+    most = [jnp.max(v, axis=0, keepdims=True) for v in most]
+    fine = (most[0] <= NEAR_LIMIT) & (jnp.maximum(most[1], most[2]) <= FAR_LIMIT)
+    flag_out[0, 0] = jnp.sum(jnp.where(lane1 & fine, 1.0, 0.0))
+    field[...] = deposit(STEPS)
+    mine = lax.broadcasted_iota(jnp.int32, (NGY, TILE), 1) == mx * NGY + my
+    planes = [jnp.where(mine, pltpu.roll(field[gxs_back[i]], my, 0), 0.0) for i in range(NGX)]
+    heat_out[0] = jnp.sum(jnp.stack(planes), axis=2)
     for copy in stores:
         copy.wait()
 
@@ -462,22 +560,30 @@
     hbm = pl.BlockSpec(memory_space=pltpu.HBM)
     vmem = pl.BlockSpec(memory_space=pltpu.VMEM)
     total = len(OFFSETS)
-    tables = lane_tables()
-    u, v, heat, flag = pl.pallas_call(
+    u, v, heat, flag, heat_same, pairs_same = pl.pallas_call(
         body,
         out_shape=(
             jax.ShapeDtypeStruct(brick, F32),
             jax.ShapeDtypeStruct(brick, F32),
             jax.ShapeDtypeStruct((1, NGX, NGY), F32),
             jax.ShapeDtypeStruct((1, 1), F32),
+            jax.ShapeDtypeStruct((NGX, NGY), F32),
+            jax.ShapeDtypeStruct((2, PAIRS), jnp.int32),
         ),
-        in_specs=[hbm] * 5 + [vmem, hbm],
-        out_specs=(hbm, hbm, vmem, pl.BlockSpec(memory_space=pltpu.SMEM)),
+        in_specs=[hbm] * 6,
+        out_specs=(hbm, hbm, vmem, pl.BlockSpec(memory_space=pltpu.SMEM), hbm, hbm),
         scratch_shapes=[
             pltpu.VMEM((STEPS + 1, 4, OWN, TILE), F32),
-            pltpu.VMEM((STEPS + 1, 4, OWN, TILE), F32),
-            pltpu.VMEM((STEPS, 8, 4, OWN, TILE), F32),
+            pltpu.VMEM((STEPS + 1, 2, OWN, TILE), F32),
+            pltpu.VMEM((STEPS, 2, 4, 12, TILE), F32),
+            pltpu.VMEM((STEPS, 8, OWN, TILE), F32),
+            pltpu.VMEM((8, TILE), F32),
+            pltpu.VMEM((NGX, NGY, TILE), F32),
+            pltpu.VMEM((NGX, NGY, TILE), F32),
             pltpu.VMEM((STEPS + 1, NGX, NGY, TILE), F32),
+            pltpu.VMEM((STEPS + 1, NGX, NGY, TILE), F32),
+            pltpu.VMEM((len(TERMS), 8, TILE), F32),
+            pltpu.VMEM((8, TILE), F32),
             pltpu.VMEM((STEPS + 1, 8, TILE), F32),
             pltpu.VMEM((4, FLAT, TILE), F32),
             pltpu.VMEM((len(SHIFTS), 4, FLAT, TILE), F32),
@@ -488,21 +594,23 @@
             pltpu.VMEM((NGX, NGY, TILE), F32),
             pltpu.VMEM((2, 18, 8, TILE), F32),
             pltpu.VMEM((2, 6, 8, TILE), F32),
-            pltpu.VMEM((1, NGX, NGY), F32),
-            pltpu.VMEM((1, 1, 2, PAIRS), jnp.int32),
-            pltpu.VMEM(tables.shape, jnp.int32),
+            pltpu.VMEM((NGX, NGY), F32),
+            pltpu.VMEM((2, PAIRS), jnp.int32),
+            pltpu.SMEM((1, 1), jnp.int32),
+            pltpu.VMEM((TABLES, 8, TILE), jnp.int32),
             pltpu.SemaphoreType.DMA((15 + 4 * STEPS,)),
             pltpu.SemaphoreType.DMA((STEPS, 8)),
             pltpu.SemaphoreType.DMA((STEPS, 8)),
             pltpu.SemaphoreType.DMA((STEPS + 1,)),
             pltpu.SemaphoreType.DMA((STEPS + 1,)),
-            pltpu.VMEM((8, TILE), F32),
+            pltpu.SemaphoreType.DMA((STEPS + 1,)),
+            pltpu.VMEM((NGX * NGY, TILE), F32),
         ],
         compiler_params=pltpu.CompilerParams(
-            collective_id=0, has_side_effects=True, vmem_limit_bytes=40 << 20
+            collective_id=0, has_side_effects=True, vmem_limit_bytes=60 << 20
         ),
-    )(turn(displacement), turn(velocity), turn(noise), electron_temp, pair_list, pair_count, jnp.asarray(tables))
-    return turn(u), turn(v), heat, flag
+    )(turn(displacement), turn(velocity), turn(noise), electron_temp[0], pair_list[0, 0], pair_count)
+    return (turn(u), turn(v), heat), flag, (heat_same[None], pairs_same[None, None])
 
 
 def padded_2(values, sides, width):
@@ -606,8 +714,11 @@
 
 
 def per_device(*arguments):
-    *results, flag = fast(*arguments)
-    return lax.cond(flag[0, 0] > 0.5, lambda: tuple(results), lambda: slow(*arguments))
+    results, flag, (heat, pairs) = fast(*arguments)
+    displacement, velocity, noise, _, _, count = arguments
+    return lax.cond(
+        flag[0, 0] > 0.5, lambda: results, lambda: slow(displacement, velocity, noise, heat, pairs, count)
+    )
 
 
 def solution(mesh):

time: 55.1 us -> 50.6 us (0.918)
  Pallas kernels: 49.1 us -> 46.3 us
  local copies, waits for them, and re-layouts: 3.6 us -> 1.83 us
    pallas_call x1, Pallas kernels: 49.1 us -> 46.3 us  [fast(): pl.pallas_call(body, out_shape=(jax.ShapeDtypeStruct(brick, F32), jax.Sha...]
    unnamed x13 -> x7, local copies, waits for them, and re-layouts: 3.6 us -> 1.83 us
where the time goes in v3:
time: 50.6 us; the launch traced here: 50.3 us
  Pallas kernels  46.3 us (92%)
  between operations  2.01 us (4%)
  local copies, waits for them, and re-layouts  1.83 us (4%)
    pallas_call x1, Pallas kernels, fast(): pl.pallas_call(body, out_shape=(jax.ShapeDtypeStruct(brick, F32), jax.Sha...  46.3 us
    unnamed x7, local copies, waits for them, and re-layouts  1.83 us

profile of v3, /device:TPU:1, one launch (start us, length us, event | category | flops | bytes accessed | tf_op | source)
XLA Modules:
  0.0 50.3 jit_solution(6474185261498077385)
XLA Ops:
  1.3 0.0 copy-start.2
  1.3 46.3 %shard_map.95 = (f32[3,2,3,2,128]{4,3,2,1,0:T(2,128)S(1)}, f32[3,2,3,2,128]{4,3,2,1,0:T(2,128)S(1)}, f32[1,8,16]{2,1,0:T(8,128)S(1)}, f32[1,1]{1,0:T(1,128)}, f32[8,16]{1,0:T(8,128)S(1)}, /*index=5*/s32[2,324]{1,0:T(2,128)S(1)}) custom-call(f32[3,2,3,2,128]{4,3,2,1,0:T(2,128)} %bitcast.156, f32[3,2,3,2,128]{4,3,2,1,0:T(2,128)} %bitcast.157, ...), custom_call_target="tpu_custom_call" | custom-call | tf_op jit(solution)/shard_map/pallas_call | solution.py:563
  47.6 0.0 copy-start.1
  48.3 0.0 copy-done.2
  48.3 0.0 copy-done.1
  48.3 0.2 conditional.1
  48.5 0.6 %copy.151 = f32[3,2,2,3,128]{4,2,3,1,0:T(2,128)} copy(f32[3,2,2,3,128]{4,2,3,1,0:T(2,128)S(1)} %get-tuple-element.1799) | data formatting | bytes 36864
  49.1 0.6 %copy.152 = f32[3,2,2,3,128]{4,2,3,1,0:T(2,128)} copy(f32[3,2,2,3,128]{4,2,3,1,0:T(2,128)S(1)} %get-tuple-element.1800) | data formatting | bytes 36864
  49.8 0.6 %copy.153 = f32[1,8,16]{2,1,0:T(8,128)} copy(f32[1,8,16]{2,1,0:T(8,128)S(1)} %get-tuple-element.1801) | data formatting | bytes 1024
  (1 shorter events, 0.0 us)
Async XLA Ops:
  1.3 47.0 %copy-start.2 = (f32[3,2,2,3,128]{4,2,3,1,0:T(2,128)S(1)}, f32[3,2,2,3,128]{4,2,3,1,0:T(2,128)}, u32[]{:S(2)}) copy-start(f32[3,2,2,3,128]{4,2,3,1,0:T(2,128)} %param.18) | copy-start | bytes 55300
  47.6 0.7 %copy-start.1 = (f32[3,2,2,3,128]{4,2,3,1,0:T(2,128)S(1)}, f32[3,2,2,3,128]{4,2,3,1,0:T(2,128)}, u32[]{:S(2)}) copy-start(f32[3,2,2,3,128]{4,2,3,1,0:T(2,128)} %param.17) | copy-start | bytes 55300

commit v4 on v3

--- a/solution.py
+++ b/solution.py
@@ -29,7 +29,7 @@
 PAD = 16
 ROWS = 48
 FLAT = PAD + ROWS + PAD
-FIRST, BLOCKS = 6, 5
+FIRST, BLOCKS = 4, 5
 
 OFFSETS = sorted(
     (
@@ -115,8 +115,8 @@
 
 def body(
     u_in, v_in, noise, heat_in, pairs_in, count,
-    u_out, v_out, heat_out, flag_out, heat_same, pairs_same,
-    own, packed, arrive_x, arrive_y, top, grid, grid_turned, near, far, weigh, column, row, win, shifted, mask, live_win, vel, kick, field,
+    u_out, v_out, heat_out, flag_out, heat_same, pairs_same, u_same, v_same,
+    own, packed, arrive_x, arrive_y, top, grid, grid_turned, near, far, weigh, column, row, win, shifted, mask, terms, live_win, vel, kick, field,
     raw, back, heat, pairs, live_count, lanes,
     in_sem, halo_send, halo_recv, all_send, all_recv, far_recv, junk,
 ):
@@ -343,26 +343,28 @@
             mine = [win[k, r : r + 8] for k in range(3)]
             density = zero8
             for o in range(total):
-                _, distance, _ = pair(o, r, mine)
+                delta, distance, inverse = pair(o, r, mine)
                 gap = jnp.minimum(distance - RC, 0.0)
-                density = density + mask[o, 8 * block : 8 * block + 8] * (gap * gap)
+                live = mask[o, 8 * block : 8 * block + 8]
+                held = live * gap
+                density = density + held * gap
+                if 0 < block < BLOCKS - 1:
+                    close = jnp.minimum(distance - RP, 0.0)
+                    quad = (2 * C0 - RP * C1) + distance * ((3 * C1 - 2 * RP * C2) + (4 * C2) * distance)
+                    terms[o, block - 1, 0] = (close * quad) * (live * inverse)
+                    terms[o, block - 1, 1] = held * inverse
+                    for k in range(3):
+                        terms[o, block - 1, 2 + k] = delta[k]
             win[3, r : r + 8] = -EMBED * lax.rsqrt(density)
         stage(total, 3)
         forces = []
         for block in range(OWN // 8):
             r = PAD + 12 + 8 * block
-            q = 12 - FIRST + 8 * block
-            mine = [win[k, r : r + 8] for k in range(3)]
             slope = win[3, r : r + 8]
             total_force = [zero8] * 3
             for o in range(total):
-                delta, distance, inverse = pair(o, r, mine)
-                gap = jnp.minimum(distance - RC, 0.0)
-                close = jnp.minimum(distance - RP, 0.0)
-                quad = (2 * C0 - RP * C1) + distance * ((3 * C1 - 2 * RP * C2) + (4 * C2) * distance)
-                scalar = close * quad + (slope + neighbour(o, 3, r)) * gap
-                scalar = scalar * inverse * mask[o, q : q + 8]
-                total_force = [f - scalar * d for f, d in zip(total_force, delta)]
+                scalar = terms[o, block, 0] + (slope + neighbour(o, 3, r)) * terms[o, block, 1]
+                total_force = [f - scalar * terms[o, block, 2 + k] for k, f in enumerate(total_force)]
             forces.append([jnp.where(inside, f, 0.0) for f in total_force])
         return forces
 
@@ -527,6 +529,8 @@
     stores = [
         pltpu.make_async_copy(heat, heat_same, in_sem.at[1]),
         pltpu.make_async_copy(pairs, pairs_same, in_sem.at[0]),
+        pltpu.make_async_copy(u_in, u_same, in_sem.at[15]),
+        pltpu.make_async_copy(v_in, v_same, in_sem.at[16]),
     ]
     for ix in range(2):
         for iy in range(2):
@@ -560,7 +564,7 @@
     hbm = pl.BlockSpec(memory_space=pltpu.HBM)
     vmem = pl.BlockSpec(memory_space=pltpu.VMEM)
     total = len(OFFSETS)
-    u, v, heat, flag, heat_same, pairs_same = pl.pallas_call(
+    u, v, heat, flag, heat_same, pairs_same, u_same, v_same = pl.pallas_call(
         body,
         out_shape=(
             jax.ShapeDtypeStruct(brick, F32),
@@ -569,9 +573,11 @@
             jax.ShapeDtypeStruct((1, 1), F32),
             jax.ShapeDtypeStruct((NGX, NGY), F32),
             jax.ShapeDtypeStruct((2, PAIRS), jnp.int32),
+            jax.ShapeDtypeStruct(brick, F32),
+            jax.ShapeDtypeStruct(brick, F32),
         ),
         in_specs=[hbm] * 6,
-        out_specs=(hbm, hbm, vmem, pl.BlockSpec(memory_space=pltpu.SMEM), hbm, hbm),
+        out_specs=(hbm, hbm, vmem, pl.BlockSpec(memory_space=pltpu.SMEM), hbm, hbm, hbm, hbm),
         scratch_shapes=[
             pltpu.VMEM((STEPS + 1, 4, OWN, TILE), F32),
             pltpu.VMEM((STEPS + 1, 2, OWN, TILE), F32),
@@ -588,6 +594,7 @@
             pltpu.VMEM((4, FLAT, TILE), F32),
             pltpu.VMEM((len(SHIFTS), 4, FLAT, TILE), F32),
             pltpu.VMEM((total, 8 * BLOCKS, TILE), F32),
+            pltpu.VMEM((total, OWN // 8, 5, 8, TILE), F32),
             pltpu.VMEM((FLAT, TILE), F32),
             pltpu.VMEM((3, OWN, TILE), F32),
             pltpu.VMEM((STEPS, 3, OWN, TILE), F32),
@@ -610,7 +617,7 @@
             collective_id=0, has_side_effects=True, vmem_limit_bytes=60 << 20
         ),
     )(turn(displacement), turn(velocity), turn(noise), electron_temp[0], pair_list[0, 0], pair_count)
-    return (turn(u), turn(v), heat), flag, (heat_same[None], pairs_same[None, None])
+    return (turn(u), turn(v), heat), flag, (turn(u_same), turn(v_same), heat_same[None], pairs_same[None, None])
 
 
 def padded_2(values, sides, width):
@@ -714,8 +721,8 @@
 
 
 def per_device(*arguments):
-    results, flag, (heat, pairs) = fast(*arguments)
-    displacement, velocity, noise, _, _, count = arguments
+    results, flag, (displacement, velocity, heat, pairs) = fast(*arguments)
+    noise, count = arguments[2], arguments[5]
     return lax.cond(
         flag[0, 0] > 0.5, lambda: results, lambda: slow(displacement, velocity, noise, heat, pairs, count)
     )

time: 50.6 us -> 50.4 us (level)
    unnamed x7 -> x3, local copies, waits for them, and re-layouts: 1.83 us -> 1.81 us
where the time goes in v4:
time: 50.4 us; the launch traced here: 50.2 us
  Pallas kernels  46.2 us (92%)
  between operations  1.99 us (4%)
  local copies, waits for them, and re-layouts  1.81 us (4%)
    pallas_call x1, Pallas kernels, fast(): pl.pallas_call(body, out_shape=(jax.ShapeDtypeStruct(brick, F32), jax.Sha...  46.2 us
    unnamed x3, local copies, waits for them, and re-layouts  1.81 us

profile of v4, /device:TPU:1, one launch (start us, length us, event | category | flops | bytes accessed | tf_op | source)
XLA Modules:
  0.0 50.2 jit_solution(3385334982856399121)
XLA Ops:
  1.3 46.2 %shard_map.95 = (f32[3,2,3,2,128]{4,3,2,1,0:T(2,128)S(1)}, f32[3,2,3,2,128]{4,3,2,1,0:T(2,128)S(1)}, f32[1,8,16]{2,1,0:T(8,128)S(1)}, f32[1,1]{1,0:T(1,128)}, f3...) custom-call(f32[3,2,3,2,128]{4,3,2,1,0:T(2,128)} %bitcast.163, ...), custom_call_target="tpu_custom_call" | custom-call | tf_op jit(solution)/shard_map/pallas_call | solution.py:567
  48.2 0.2 conditional.1
  48.4 0.6 %copy.151 = f32[3,2,2,3,128]{4,2,3,1,0:T(2,128)} copy(f32[3,2,2,3,128]{4,2,3,1,0:T(2,128)S(1)} %get-tuple-element.1803) | data formatting | bytes 36864
  49.0 0.6 %copy.152 = f32[3,2,2,3,128]{4,2,3,1,0:T(2,128)} copy(f32[3,2,2,3,128]{4,2,3,1,0:T(2,128)S(1)} %get-tuple-element.1804) | data formatting | bytes 36864
  49.6 0.6 %copy.153 = f32[1,8,16]{2,1,0:T(8,128)} copy(f32[1,8,16]{2,1,0:T(8,128)S(1)} %get-tuple-element.1805) | data formatting | bytes 1024
  (1 shorter events, 0.0 us)
